TPU v7x, 128 devices: a whole 4x4x4 slice. The times are simulated.
128 devices in a mesh: exp: 32 (over y, x, core), imp: 4 (over z).
Axes of the slice: x: 4, y: 4, z: 4, core: 2. Of those that a mesh axis runs over, the one named last changes fastest.
Arguments:
- flows: bfloat16 [512, 256, 256], P(('exp', 'imp')), may hold values from 0 to 8, as said below
- routing: int32 [128, 4, 1], P(('exp', 'imp')), may hold values from -1 to 3, as said below
- tile_block: int32 [512], P(('exp', 'imp')), may hold values from 0 to 7, as said below
- exp_country: int32 [16384], P('exp'), may hold values from 0 to 127, never falling along the last dimension, each value on 1 to 256 neighbouring positions
- imp_country: int32 [4096], P('imp'), may hold values from 0 to 127, never falling along the last dimension, each value on 1 to 64 neighbouring positions
Outputs:
- exporter_effects: float32 [16384], P('exp')
- importer_effects: float32 [4096], P('imp')
- pair_effects: float32 [128, 128], replicated
Inputs may be any that keep to these rules, and one draw needn't show every extreme that they name: `routing`: entry [d, t, s] names a slot of device d routed to imp index t, or is -1. Each slot is named at most once. The devices of one exp index route at most 3 named slots to each imp index in all, and exactly 3 to some imp index of every exp index; each entry names at most one slot, and some entry of some device does name one; in every exp index some device names all 4 of its slots. `tile_block`: r * 4 + c for the slot's local exporter block r and local importer block c; distinct within a device. `exp_country`: never falls along the exporter-years; every country has 1 to 256 of them. `imp_country`: never falls along the importer-years; every country has 1 to 64 of them. Positive flows.
All inputs are finite; a program needn't handle non-finite values.
Results may differ from a plain program's by a relative error of at most 0.0003.
Values may be sent and summed in bfloat16 or wider, within the bound.
A program may use at most 64 MiB of HBM per device.

v0:
```python
import jax
import jax.numpy as jnp
from jax import lax
from jax.sharding import PartitionSpec as P

NCE = 128
NCI = 128
NEWTON = 2
CG = 2


ridge_weight = 64.0


def combine(anchor, factor, change):
    return tuple((current + factor * addend for current, addend in zip(anchor, change)))


def per_device(flows, routing, tile_block, exp_country, imp_country):
    slots_home = flows.shape[0]
    tile_side = flows.shape[1]
    imp_place = lax.axis_index("imp")
    exp_place = lax.axis_index("exp")
    row_blocks = exp_country.shape[0] // tile_side
    col_local = imp_country.shape[0] // tile_side
    routes = routing[0]
    numbers = jnp.arange(slots_home, dtype=jnp.int32)
    is_live = jnp.any(routes[None, :, :] == numbers[:, None, None], axis=(1, 2))
    row_block = tile_block // col_local
    col_block = tile_block % col_local
    within = jnp.arange(tile_side, dtype=jnp.int32)
    row_country = exp_country[row_block[:, None] * tile_side + within[None, :]]
    col_tile_country = imp_country[col_block[:, None] * tile_side + within[None, :]]
    row_hot = (row_country[:, :, None] == jnp.arange(NCE, dtype=jnp.int32)[None, None, :]).astype(
        jnp.float32
    )
    col_hot = (
        col_tile_country[:, :, None] == jnp.arange(NCI, dtype=jnp.int32)[None, None, :]
    ).astype(jnp.float32)
    block_rows = (row_block[:, None] == jnp.arange(row_blocks, dtype=jnp.int32)[None, :]).astype(
        jnp.float32
    )
    block_cols = (col_block[:, None] == jnp.arange(col_local, dtype=jnp.int32)[None, :]).astype(
        jnp.float32
    )
    live_mask = is_live[:, None, None]
    first_exp = exp_place == 0
    first_imp = imp_place == 0
    highest = lax.Precision.HIGHEST

    def expand(effects):
        exporter_rows = effects[0].reshape(row_blocks, tile_side)[row_block]
        importer_rows = effects[1].reshape(col_local, tile_side)[col_block]
        pair_table = effects[2]
        row_pairs = jnp.einsum("kin,nm->kim", row_hot, pair_table, precision=highest)
        looked_up = jnp.einsum("kim,kjm->kij", row_pairs, col_hot, precision=highest)
        return exporter_rows[:, :, None] + importer_rows[:, None, :] + looked_up

    def collect(weighted):
        part_rows = jnp.einsum(
            "kr,ki->ri", block_rows, jnp.sum(weighted, axis=2), precision=highest
        ).reshape(-1)
        part_cols = jnp.einsum(
            "kc,kj->cj", block_cols, jnp.sum(weighted, axis=1), precision=highest
        ).reshape(-1)
        half_pairs = jnp.einsum("kin,kij->knj", row_hot, weighted, precision=highest)
        part_pairs = jnp.einsum("knj,kjm->nm", half_pairs, col_hot, precision=highest)
        exporter_total = lax.psum(part_rows, "imp")
        importer_total = lax.psum(part_cols, "exp")
        pair_total = lax.psum(part_pairs, ("exp", "imp"))
        return (exporter_total, importer_total, pair_total)

    def local_part(left_vec, right_vec):
        exporter_term = jnp.sum(left_vec[0] * right_vec[0])
        importer_term = jnp.sum(left_vec[1] * right_vec[1])
        pair_term = jnp.sum(left_vec[2] * right_vec[2])
        local_sum = jnp.where(first_imp, exporter_term, 0.0) + jnp.where(
            first_exp, importer_term, 0.0
        )
        local_sum = local_sum + jnp.where(first_exp & first_imp, pair_term, 0.0)
        return local_sum

    def inner_product(left_vec, right_vec):
        return lax.psum(local_part(left_vec, right_vec), ("exp", "imp"))

    pair_rows = NCE
    effects = (
        jnp.zeros((row_blocks * tile_side,), jnp.float32),
        jnp.zeros((col_local * tile_side,), jnp.float32),
        jnp.zeros((pair_rows, NCI), jnp.float32),
    )
    for newton in range(NEWTON):
        mean_rate = jnp.where(live_mask, jnp.exp(expand(effects)), 0.0)
        gradient = collect(jnp.where(live_mask, flows.astype(jnp.float32) - mean_rate, 0.0))
        residual = combine(gradient, -ridge_weight, effects)
        update = tuple((jnp.zeros_like(current) for current in effects))
        direction = residual
        norm_now = inner_product(residual, residual)
        for cg_sweep in range(CG):
            image_vec = combine(collect(mean_rate * expand(direction)), ridge_weight, direction)
            step_size = norm_now / inner_product(direction, image_vec)
            update = combine(update, step_size, direction)
            residual = combine(residual, -step_size, image_vec)
            norm_next = inner_product(residual, residual)
            direction = combine(residual, norm_next / norm_now, direction)
            norm_now = norm_next
        effects = combine(effects, 1.0, update)
    return (effects[0], effects[1], effects[2])


def solution(mesh):
    placed = (
        P(("exp", "imp"), None, None),
        P(("exp", "imp"), None, None),
        P(("exp", "imp")),
        P("exp"),
        P("imp"),
    )
    return jax.shard_map(
        per_device, mesh=mesh, in_specs=placed, out_specs=(P("exp"), P("imp"), P()), check_vma=False
    )
```

profile of v0, /device:TPU:1, one launch (start us, length us, event | category | flops | bytes accessed | tf_op | source)
XLA Modules:
  0.0 1648.1 jit_solution(12375132039694801834)
XLA Ops:
  8.6 4.5 gather_fusion.3
  13.3 6.9 gather_fusion.2
  22.0 1.4 fusion.73
  23.4 0.7 fusion.20
  24.1 1.1 convolution_bitcast_fusion.5
  25.9 10.6 psum.182
  37.0 65.0 %psum.183 = f32[1024]{0:T(1024)S(1)} all-reduce(f32[1024]{0:T(1024)S(1)} %bitcast.100), channel_id=1, replica_groups=mesh['exp'=32,'imp'=4] {'exp'}, use_global_device_ids=true, to_apply=%region_5.6 | all-reduce | flops 1024 | bytes 8192 | tf_op jit(solution)/shard_map/psum | solution.py:69
  102.6 65.8 %all-reduce.9.cloned.1.call-done = f32[128,128]{1,0:T(8,128)} async-done(((f32[128,128]{1,0:T(8,128)}), f32[128,128]{1,0:T(8,128)}) %all-reduce.9.cloned.1.call-update) | async-done | bytes 65552 | tf_op jit(solution)/shard_map/psum | solution.py:70
  168.4 1.4 fusion.19
  169.8 1.3 fusion.78
  171.4 60.2 %psum.187 = f32[1024]{0:T(1024)S(1)} all-reduce(f32[1024]{0:T(1024)S(1)} %bitcast.103), channel_id=1, replica_groups=mesh['exp'=32,'imp'=4] {'exp'}, use_global_device_ids=true, to_apply=%region_14.15 | all-reduce | flops 1024 | bytes 8192 | tf_op jit(solution)/shard_map/psum | solution.py:69
  232.5 8.4 psum.186
  241.4 1.1 convolution_bitcast_fusion.4
  245.8 135.7 %all-reduce.11.cloned.1.call-done = f32[128,128]{1,0:T(8,128)} async-done(((f32[128,128]{1,0:T(8,128)}), f32[128,128]{1,0:T(8,128)}) %all-reduce.11.cloned.1.call-update) | async-done | bytes 65552 | tf_op jit(solution)/shard_map/psum | solution.py:70
  381.5 1.5 multiply_reduce_fusion.6
  384.3 63.3 %all-reduce.1 = (f32[]{:T(128)}, f32[]{:T(128)}) all-reduce(f32[]{:T(128)S(6)} %add.411, f32[]{:T(128)S(6)} %add.420), channel_id=1, replica_groups=mesh['exp'=32,'imp'=4] {'exp','imp'}, use_global_device_ids=true, to_apply=%region_9.10 | all-reduce | flops 2 | bytes 16 | tf_op jit(solution)/shard_map/psum | solution.py:84
  450.2 0.7 multiply_reduce_fusion.5
  452.9 62.8 %psum.190 = f32[]{:T(128)} all-reduce(f32[]{:T(128)S(6)} %add.425), channel_id=1, replica_groups=mesh['exp'=32,'imp'=4] {'exp','imp'}, use_global_device_ids=true, to_apply=%region_22.23 | all-reduce | flops 1 | bytes 8 | tf_op jit(solution)/shard_map/psum | solution.py:84
  518.7 1.3 fusion.77
  520.3 62.7 %psum.192 = f32[1024]{0:T(1024)S(1)} all-reduce(f32[1024]{0:T(1024)S(1)} %bitcast.104), channel_id=1, replica_groups=mesh['exp'=32,'imp'=4] {'exp'}, use_global_device_ids=true, to_apply=%region_27.28 | all-reduce | flops 1024 | bytes 8192 | tf_op jit(solution)/shard_map/psum | solution.py:69
  583.9 8.0 psum.191
  592.4 1.1 convolution_bitcast_fusion.3
  595.5 135.0 %all-reduce.13.cloned.1.call-done = f32[128,128]{1,0:T(8,128)} async-done(((f32[128,128]{1,0:T(8,128)}), f32[128,128]{1,0:T(8,128)}) %all-reduce.13.cloned.1.call-update) | async-done | bytes 65552 | tf_op jit(solution)/shard_map/psum | solution.py:70
  730.5 1.5 multiply_reduce_fusion.4
  732.7 63.5 %psum.194 = f32[]{:T(128)} all-reduce(f32[]{:T(128)S(6)} %add.437), channel_id=1, replica_groups=mesh['exp'=32,'imp'=4] {'exp','imp'}, use_global_device_ids=true, to_apply=%region_31.32 | all-reduce | flops 1 | bytes 8 | tf_op jit(solution)/shard_map/psum | solution.py:84
  799.3 1.4 fusion.70
  800.9 62.8 %psum.196 = f32[1024]{0:T(1024)S(1)} all-reduce(f32[1024]{0:T(1024)S(1)} %bitcast.105), channel_id=1, replica_groups=mesh['exp'=32,'imp'=4] {'exp'}, use_global_device_ids=true, to_apply=%region_36.37 | all-reduce | flops 1024 | bytes 8192 | tf_op jit(solution)/shard_map/psum | solution.py:69
  864.0 7.0 psum.195
  870.9 0.7 fusion.14
  871.7 1.1 convolution_bitcast_fusion.2
  874.0 136.7 %all-reduce.15.cloned.1.call-done = f32[128,128]{1,0:T(8,128)} async-done(((f32[128,128]{1,0:T(8,128)}), f32[128,128]{1,0:T(8,128)}) %all-reduce.15.cloned.1.call-update) | async-done | bytes 65552 | tf_op jit(solution)/shard_map/psum | solution.py:70
  1010.7 0.9 multiply_add_fusion.3
  1012.2 1.3 fusion.76
  1013.7 60.1 %psum.200 = f32[1024]{0:T(1024)S(1)} all-reduce(f32[1024]{0:T(1024)S(1)} %bitcast.106), channel_id=1, replica_groups=mesh['exp'=32,'imp'=4] {'exp'}, use_global_device_ids=true, to_apply=%region_45.46 | all-reduce | flops 1024 | bytes 8192 | tf_op jit(solution)/shard_map/psum | solution.py:69
  1074.7 8.4 psum.199
  1083.7 1.1 convolution_bitcast_fusion.1
  1088.0 135.7 %all-reduce.17.cloned.1.call-done = f32[128,128]{1,0:T(8,128)} async-done(((f32[128,128]{1,0:T(8,128)}), f32[128,128]{1,0:T(8,128)}) %all-reduce.17.cloned.1.call-update) | async-done | bytes 65552 | tf_op jit(solution)/shard_map/psum | solution.py:70
  1223.7 1.5 multiply_reduce_fusion.2
  1226.6 63.3 %all-reduce = (f32[]{:T(128)}, f32[]{:T(128)}) all-reduce(f32[]{:T(128)S(6)} %add.449, f32[]{:T(128)S(6)} %add.458), channel_id=1, replica_groups=mesh['exp'=32,'imp'=4] {'exp','imp'}, use_global_device_ids=true, to_apply=%region_40.41 | all-reduce | flops 2 | bytes 16 | tf_op jit(solution)/shard_map/psum | solution.py:84
  1292.4 0.7 multiply_reduce_fusion.1
  1295.1 62.8 %psum.203 = f32[]{:T(128)} all-reduce(f32[]{:T(128)S(6)} %add.463), channel_id=1, replica_groups=mesh['exp'=32,'imp'=4] {'exp','imp'}, use_global_device_ids=true, to_apply=%region_53.54 | all-reduce | flops 1 | bytes 8 | tf_op jit(solution)/shard_map/psum | solution.py:84
  1361.0 1.3 fusion.75
  1362.5 62.7 %psum.205 = f32[1024]{0:T(1024)S(1)} all-reduce(f32[1024]{0:T(1024)S(1)} %bitcast.107), channel_id=1, replica_groups=mesh['exp'=32,'imp'=4] {'exp'}, use_global_device_ids=true, to_apply=%region_58.59 | all-reduce | flops 1024 | bytes 8192 | tf_op jit(solution)/shard_map/psum | solution.py:69
  1426.0 8.0 psum.204
  1434.6 1.1 convolution_bitcast_fusion
  1437.6 135.1 %all-reduce.19.cloned.1.call-done = f32[128,128]{1,0:T(8,128)} async-done(((f32[128,128]{1,0:T(8,128)}), f32[128,128]{1,0:T(8,128)}) %all-reduce.19.cloned.1.call-update) | async-done | bytes 65552 | tf_op jit(solution)/shard_map/psum | solution.py:70
  1572.7 1.5 multiply_reduce_fusion
  1574.8 63.3 %psum.207 = f32[]{:T(128)} all-reduce(f32[]{:T(128)S(6)} %add.475), channel_id=1, replica_groups=mesh['exp'=32,'imp'=4] {'exp','imp'}, use_global_device_ids=true, to_apply=%region_62.63 | all-reduce | flops 1 | bytes 8 | tf_op jit(solution)/shard_map/psum | solution.py:84
  (122 shorter events, 26.4 us)
Async XLA Ops:
  7.2 1.5 copy-start
  7.2 0.7 copy-start.7
  7.2 161.2 %all-reduce.9.cloned.1.call-start = ((), (), s32[]{:S(2)}) async-start(), calls=%async_computation | async-start | bytes 131072 | tf_op jit(solution)/shard_map/psum | solution.py:70
  7.8 0.7 copy-start.6
  8.6 4.7 copy-start.1
  20.2 1.8 copy-start.3
  25.3 356.2 %all-reduce.11.cloned.1.call-start = ((), (), s32[]{:S(2)}) async-start(), calls=%async_computation.1 | async-start | bytes 131072 | tf_op jit(solution)/shard_map/psum | solution.py:70
  242.5 138.9 %copy-start.2 = (f32[128,128]{1,0:T(8,128)S(1)}, f32[128,128]{1,0:T(8,128)}, u32[]{:S(2)}) copy-start(f32[128,128]{1,0:T(8,128)} %all-reduce.9.cloned.1.call-done) | copy-start | bytes 196612
  242.6 488.0 %all-reduce.13.cloned.1.call-start = ((), (), s32[]{:S(2)}) async-start(), calls=%async_computation.2 | async-start | bytes 131072 | tf_op jit(solution)/shard_map/psum | solution.py:70
  381.5 68.7 %copy-start.4 = (f32[128,128]{1,0:T(8,128)S(1)}, f32[128,128]{1,0:T(8,128)}, u32[]{:S(2)}) copy-start(f32[128,128]{1,0:T(8,128)} %all-reduce.11.cloned.1.call-done) | copy-start | bytes 196612
  593.6 417.1 %all-reduce.15.cloned.1.call-start = ((), (), s32[]{:S(2)}) async-start(), calls=%async_computation.3 | async-start | bytes 131072 | tf_op jit(solution)/shard_map/psum | solution.py:70
  872.8 350.9 %all-reduce.17.cloned.1.call-start = ((), (), s32[]{:S(2)}) async-start(), calls=%async_computation.4 | async-start | bytes 131072 | tf_op jit(solution)/shard_map/psum | solution.py:70
  1084.8 487.8 %all-reduce.19.cloned.1.call-start = ((), (), s32[]{:S(2)}) async-start(), calls=%async_computation.5 | async-start | bytes 131072 | tf_op jit(solution)/shard_map/psum | solution.py:70
  1223.7 68.7 %copy-start.5 = (f32[128,128]{1,0:T(8,128)S(1)}, f32[128,128]{1,0:T(8,128)}, u32[]{:S(2)}) copy-start(f32[128,128]{1,0:T(8,128)} %all-reduce.17.cloned.1.call-done) | copy-start | bytes 196612
Sparse Core Ops, SparseCore 0:
  25.4 142.9 all-reduce.8
  242.7 138.7 all-reduce.10
  593.7 136.7 all-reduce.12
  873.0 137.7 all-reduce.14
  1085.0 138.7 all-reduce.16
  1435.8 136.7 all-reduce.18
where the time goes:
time: 1650 us
  blocking collectives  802 us (49%)
  waiting for transfers between devices  744 us (45%)
  between operations  38 us (2%)
  matrix products  25.8 us (2%)
  local copies, waits for them, and re-layouts  19.6 us (1%)
  other arithmetic  17.9 us (1%)
    psum x6, waiting for transfers between devices, collect(): pair_total = lax.psum(part_pairs, ('exp', 'imp'))  744 us
    psum x6, blocking collectives, inner_product(): return lax.psum(local_part(left_vec, right_vec), ('exp', 'imp'))  379 us
    psum x6, blocking collectives, collect(): importer_total = lax.psum(part_cols, 'exp')  373 us
    psum x6, blocking collectives, collect(): exporter_total = lax.psum(part_rows, 'imp')  50.3 us
  transfers between devices with their start and end apart: 6, of which 6 were waited for; matrix products, arithmetic and copies ran while one was open for 0% of the time, Pallas kernels for 0%

commit v1 on v0

v1 whole, which is shorter than its diff:
```python
import functools

import jax
import jax.numpy as jnp
from jax import lax
from jax.experimental import pallas as pl
from jax.experimental.pallas import tpu as pltpu
from jax.sharding import PartitionSpec as P

MESH = pl.DeviceIdType.MESH
RIDGE = 64.0
NC = 128
SIDE = 256
SLOTS = 4
F32 = jnp.float32
BF16 = jnp.bfloat16


def split(x):
    hi = x.astype(BF16)
    lo = (x - hi.astype(F32)).astype(BF16)
    return hi, lo


def dot(x, y):
    return lax.dot_general(x, y, (((1,), (0,)), ((), ())), preferred_element_type=F32)


def dot_nt(x, y):
    return lax.dot_general(x, y, (((1,), (1,)), ((), ())), preferred_element_type=F32)


def kernel(
    dims,
    routing,
    tile_block,
    flows,
    exp_ids,
    imp_ids,
    a_out,
    b_out,
    g_out,
    fbuf,
    row_t,
    row_s,
    col_t,
    col_s,
    x0,
    xq,
    mu,
    ubuf,
    vbuf,
    va,
    vb,
    r0g,
    qg,
    eg,
    own,
    gown,
    zb,
    bb,
    yb,
    hs,
    hb,
    sb,
    pb,
    rsb,
    rxb,
    gfull,
    fsem,
    zs,
    zr,
    bs,
    br,
    ys,
    yr,
    hss,
    hr,
    ss,
    sr,
    ps,
    pr,
    rss,
    rsr,
    rxs,
    rxr,
    ags,
    agr,
):
    Y, XC, Z = dims
    E, YZ = Y * XC, Y * Z
    rows_chunk = NC // YZ
    e = lax.axis_index("exp")
    m = lax.axis_index("imp")
    y = lax.div(e, XC)
    j = lax.rem(e, XC)
    p = y * Z + m

    xc_dev = [(y * XC + lax.rem(j + k, XC), m) for k in range(1, XC)]
    z_dev = [(e, lax.rem(m + k, Z)) for k in range(1, Z)]
    y_dev = [(lax.rem(y + k, Y) * XC + j, m) for k in range(1, Y)]
    yz_idx = [(lax.rem(y + ky, Y), lax.rem(m + kz, Z)) for ky in range(Y) for kz in range(Z)][1:]
    yz_dev = [(yy * XC + j, mm) for yy, mm in yz_idx]
    h_dev = [(lax.rem(e + 1, E), m), (lax.rem(e + E - 1, E), m)]

    barrier = pltpu.get_barrier_semaphore()
    greet = xc_dev + yz_dev + h_dev
    for dev in greet:
        pl.semaphore_signal(barrier, inc=1, device_id=dev, device_id_type=MESH)

    fcopy = pltpu.make_async_copy(flows, fbuf, fsem)
    fcopy.start()

    pending = []

    def push(src, dst, send_sem, recv_sem, dev):
        copy = pltpu.make_async_remote_copy(
            src_ref=src, dst_ref=dst, send_sem=send_sem, recv_sem=recv_sem, device_id=dev, device_id_type=MESH
        )
        copy.start()
        pending.append(copy)
        return copy

    def arrive(copies):
        for copy in copies:
            copy.wait_recv()

    riota = lax.broadcasted_iota(jnp.int32, (NC, NC), 0)
    ciota = lax.broadcasted_iota(jnp.int32, (NC, NC), 1)
    riota_f, ciota_f = riota.astype(F32), ciota.astype(F32)
    row_blk, col_blk, live = [], [], []
    for k in range(SLOTS):
        blk = tile_block[k]
        row_blk.append(lax.div(blk, 4))
        col_blk.append(lax.rem(blk, 4))
        hit = jnp.int32(0)
        for t in range(routing.shape[0]):
            hit = hit | jnp.where(routing[t] == k, 1, 0)
        live.append(hit)
    erow = [exp_ids[pl.ds(2 * row_blk[k] + h, 1), :] for k in range(SLOTS) for h in range(2)]
    irow = [imp_ids[pl.ds(2 * col_blk[k] + h, 1), :] for k in range(SLOTS) for h in range(2)]
    ids_t = jnp.concatenate(
        [v.astype(F32) for v in erow + irow] + [jnp.zeros((NC - 4 * SLOTS, NC), F32)], axis=0
    ).T
    for q in range(2 * SLOTS):
        k, h = divmod(q, 2)
        row_t[:, NC * q : NC * (q + 1)] = jnp.where(riota == erow[q], 1.0, 0.0).astype(BF16)
        row_s[NC * q : NC * (q + 1), :] = jnp.where(ciota_f == ids_t[:, q : q + 1], 1.0, 0.0).astype(BF16)
        hot = jnp.where(riota == irow[q], 1.0, 0.0).astype(BF16)
        col_t[k, 0:NC, NC * h : NC * (h + 1)] = hot
        col_t[k, NC : 2 * NC, NC * h : NC * (h + 1)] = hot
        col_s[NC * q : NC * (q + 1), :] = jnp.where(
            ciota_f == ids_t[:, 2 * SLOTS + q : 2 * SLOTS + q + 1], 1.0, 0.0
        ).astype(BF16)
    eids, iids = exp_ids[...].astype(F32), imp_ids[...].astype(F32)

    def least(v):
        return jnp.min(jnp.min(v, axis=0, keepdims=True), axis=1, keepdims=True)

    rf = jnp.broadcast_to(least(eids), (1, NC))
    rl = jnp.broadcast_to(-least(-eids), (1, NC))
    cf = jnp.broadcast_to(least(iids), (1, NC))
    cl = jnp.broadcast_to(-least(-iids), (1, NC))
    lane = lax.broadcasted_iota(jnp.int32, (1, NC), 1).astype(F32)
    zero_row = jnp.zeros((1, NC), F32)
    ends = jnp.concatenate(
        [jnp.where(lane == cf, 1.0, 0.0), jnp.where(lane == cl, 1.0, 0.0)] + [zero_row] * 6, axis=0
    ).astype(BF16)
    ones8 = jnp.ones((8, 2 * NC), BF16)
    row_w = [[jnp.where(row_blk[k] == c, 1.0, 0.0) for c in range(2)] for k in range(SLOTS)]
    col_w = [[jnp.where(col_blk[k] == c, 1.0, 0.0) for c in range(4)] for k in range(SLOTS)]

    def keep(k, x):
        return jnp.where(jnp.full(x.shape, live[k]) > 0, x, 0.0)

    def collect(cells):
        sums = []
        for k in range(SLOTS):
            w = cells(k)
            hi, lo = split(w)
            cs = col_s[SIDE * k : SIDE * (k + 1), :]
            vhi, vlo = split(dot(hi, cs) + dot(lo, cs))
            vbuf[SIDE * k : SIDE * (k + 1), 0:NC] = vhi
            vbuf[SIDE * k : SIDE * (k + 1), NC : 2 * NC] = vlo
            sums.append(jnp.sum(w, axis=0, keepdims=True))
        v = vbuf[...]
        wide = dot(row_t[...], v)
        table = wide[:, 0:NC] + wide[:, NC : 2 * NC]
        rsum = dot_nt(ones8, v)
        arows, brows = [], []
        for c in range(2):
            for h in range(2):
                arows.append(
                    sum(
                        row_w[k][c] * rsum[0:1, SIDE * k + NC * h : SIDE * k + NC * (h + 1)]
                        for k in range(SLOTS)
                    )
                )
        for c in range(4):
            for h in range(2):
                brows.append(sum(col_w[k][c] * sums[k][:, NC * h : NC * (h + 1)] for k in range(SLOTS)))
        return table, arows, brows

    def vec_send(r, table, arows, brows, scal):
        hi, lo = split(table)
        edge = dot_nt(ends, jnp.concatenate([hi, lo], axis=0))
        edge = edge[:, 0:NC] + edge[:, NC : 2 * NC]
        first = jnp.sum(jnp.where(riota_f == rf, table, 0.0), axis=0, keepdims=True)
        last = jnp.sum(jnp.where(riota_f == rl, table, 0.0), axis=0, keepdims=True)
        width = 8 if scal is None else 16
        bb[r, j, 0:8, :] = jnp.concatenate(brows, axis=0)
        if scal is not None:
            bb[r, j, 8:16, :] = scal
        src = bb.at[r, j, pl.ds(0, width)]
        bcopies = [push(src, src, bs.at[r, k], br.at[r, k], dev) for k, dev in enumerate(xc_dev)]
        zb[r, m, 0:8, :] = jnp.concatenate(arows + [edge[0:1], edge[1:2], first, last], axis=0)
        width = 8
        if r == 0:
            zb[r, m, 8:16, :] = jnp.concatenate([cf, cl] + [zero_row] * 6, axis=0)
            width = 16
        src = zb.at[r, m, pl.ds(0, width)]
        zcopies = [push(src, src, zs.at[r, k], zr.at[r, k], dev) for k, dev in enumerate(z_dev)]
        return zcopies, bcopies

    def vec_turn(r, zcopies, bcopies, scal):
        arrive(bcopies)
        yb[r, y] = sum(bb[r, k, 0:8, :] for k in range(XC))
        src = yb.at[r, y]
        ycopies = [push(src, src, ys.at[r, k], yr.at[r, k], dev) for k, dev in enumerate(y_dev)]
        pcopies = []
        if scal is not None:
            pcopies = scal_turn(scal, sum(bb[r, k, 8:16, :] for k in range(XC)))
        arrive(zcopies)
        edge = sum(zb[r, k, 0:8, :] for k in range(Z))
        hs[r] = jnp.concatenate([edge[6:7], edge[7:8], rf, rl] + [zero_row] * 4, axis=0)
        hcopies = [
            push(hs.at[r], hb.at[r, 0], hss.at[r, 0], hr.at[r, 0], h_dev[0]),
            push(hs.at[r], hb.at[r, 1], hss.at[r, 1], hr.at[r, 1], h_dev[1]),
        ]
        return edge[0:4], ycopies, hcopies, pcopies

    def scal_turn(s, total):
        pb[s, p] = total
        src = pb.at[s, p]
        return [push(src, src, ps.at[s, k], pr.at[s, k], dev) for k, dev in enumerate(yz_dev)]

    def scal_total(s, pcopies):
        arrive(pcopies)
        total = sum(pb[s, k] for k in range(YZ))
        return jnp.sum(total, axis=1, keepdims=True)

    def columns(r, avec):
        va[0:4, :] = avec
        tiles = [va[pl.ds(2 * row_blk[k] + h, 1), :] for k in range(SLOTS) for h in range(2)]
        prev = zb[r, lax.rem(m + Z - 1, Z), 5:6, :]
        after = zb[r, lax.rem(m + 1, Z), 4:5, :]
        return jnp.concatenate(tiles + [prev, after, jnp.zeros((NC - 10, NC), F32)], axis=0).T

    def vec_end(r, table, cols, ycopies, hcopies):
        cl_prev = zb[0, lax.rem(m + Z - 1, Z), 9:10, :]
        cf_next = zb[0, lax.rem(m + 1, Z), 8:9, :]
        table = table + jnp.where(ciota_f == cl_prev, cols[:, 8:9], 0.0)
        table = table + jnp.where(ciota_f == cf_next, cols[:, 9:10], 0.0)
        arrive(hcopies)
        rl_prev, rf_next = hb[0, 0, 3:4, :], hb[0, 1, 2:3, :]
        table = table + jnp.where(riota_f == rl_prev, hb[r, 0, 1:2, :], 0.0)
        table = table + jnp.where(riota_f == rf_next, hb[r, 1, 0:1, :], 0.0)
        arrive(ycopies)
        bvec = sum(yb[r, k] for k in range(Y))
        if r == 0:
            skip_r = jnp.where(rl_prev == rf, 1.0, 0.0)
            skip_c = jnp.where(cl_prev == cf, 1.0, 0.0)
            mine = (riota_f >= rf + skip_r) & (riota_f <= rl) & (ciota_f >= cf + skip_c) & (ciota_f <= cl)
            own[...] = jnp.where(mine, 1.0, 0.0)
        return table, bvec

    def expand(gval, cols, bvec):
        hi, lo = split(gval)
        ubuf[...] = dot(row_s[...], jnp.concatenate([hi, lo], axis=1)).astype(BF16)
        vb[...] = bvec

        def tile(k):
            brow = jnp.concatenate([vb[pl.ds(2 * col_blk[k] + h, 1), :] for h in range(2)], axis=1)
            acol = jnp.concatenate([cols[:, 2 * k + h : 2 * k + h + 1] for h in range(2)], axis=0)
            return dot(ubuf[SIDE * k : SIDE * (k + 1), :], col_t[k]) + acol + brow

        return tile

    def fold(x):
        x = jnp.sum(x.reshape(SIDE // 8, 8, SIDE), axis=0)
        return x[:, 0:NC] + x[:, NC:SIDE]

    def lanes(x):
        return jnp.sum(x, axis=0, keepdims=True)

    def inner(u, v):
        total = lanes(u[0] * v[0]) * (1.0 / Z) + lanes(u[1] * v[1]) * (1.0 / E)
        return total + lanes(own[...] * u[2] * v[2])

    effects = None
    for newton in range(2):
        r = 2 * newton
        if newton == 0:

            def cells(k):
                mu[k] = keep(k, jnp.ones((SIDE, SIDE), F32))
                return keep(k, fbuf[k].astype(F32) - 1.0)

            fcopy.wait()
        else:

            def cells(k):
                rate = keep(k, jnp.exp(c0 * x0[k] + c1 * (x0[k] - step * xq[k])))
                mu[k] = rate
                return keep(k, fbuf[k].astype(F32)) - rate

        table, arows, brows = collect(cells)
        if newton == 0:
            pl.semaphore_wait(barrier, len(greet))
        zc, bc = vec_send(r, table, arows, brows, None)
        ra, yc, hc, _ = vec_turn(r, zc, bc, None)
        if newton:
            ra = ra - RIDGE * effects[0]
        cols = columns(r, ra)
        rg, rb = vec_end(r, table, cols, yc, hc)
        if newton:
            rg = rg - RIDGE * eg[...]
            rb = rb - RIDGE * effects[1]
        r0g[...] = rg
        res = (ra, rb, rg)
        tile = expand(rg, cols, rb)
        quad = []

        def cells(k):
            x = tile(k)
            x0[k] = x
            w = mu[k] * x
            quad.append(fold(w * x))
            return w

        table, arows, brows = collect(cells)
        scal = jnp.concatenate([inner(res, res), lanes(sum(quad))] + [zero_row] * 6, axis=0)
        zc, bc = vec_send(r + 1, table, arows, brows, scal)
        qa, yc, hc, pc = vec_turn(r + 1, zc, bc, r)
        qa = qa + RIDGE * ra
        cols = columns(r + 1, qa)
        qgv, qb = vec_end(r + 1, table, cols, yc, hc)
        qgv = qgv + RIDGE * r0g[...]
        qb = qb + RIDGE * rb
        qg[...] = qgv
        tile = expand(qgv, cols, qb)
        for k in range(SLOTS):
            xq[k] = tile(k)
        total = scal_total(r, pc)
        rr = total[0:1]
        rhr = total[1:2] + RIDGE * rr
        step = rr / rhr
        quad = []
        for k in range(SLOTS):
            x = x0[k] - step * xq[k]
            quad.append(fold(mu[k] * x * x))
        qvec = (qa, qb, qg[...])
        res1 = (ra - step * qa, rb - step * qb, r0g[...] - step * qg[...])
        sb[newton, j] = jnp.concatenate(
            [inner(res1, res1), lanes(sum(quad)), inner(res1, qvec)] + [zero_row] * 5, axis=0
        )
        src = sb.at[newton, j]
        sc = [push(src, src, ss.at[newton, k], sr.at[newton, k], dev) for k, dev in enumerate(xc_dev)]
        arrive(sc)
        pc = scal_turn(r + 1, sum(sb[newton, k] for k in range(XC)))
        total = scal_total(r + 1, pc)
        rr1 = total[0:1]
        beta = rr1 / rr
        curve = total[1:2] + RIDGE * rr1 + 2.0 * beta * total[2:3] + beta * beta * rhr
        c1 = rr1 / curve
        c0 = step + c1 * beta
        moved = [
            c0 * u + c1 * v
            for u, v in zip((ra, rb, r0g[...]), (ra - step * qa, rb - step * qb, r0g[...] - step * qg[...]))
        ]
        if newton == 0:
            effects = (moved[0], moved[1])
            eg[...] = moved[2]
        else:
            a_out[...] = effects[0] + moved[0]
            b_out[...] = effects[1] + moved[1]
            gown[...] = (eg[...] + moved[2]) * own[...]

    rsb[p] = gown[pl.ds(p * rows_chunk, rows_chunk), :]
    copies = [
        push(
            gown.at[pl.ds((yy * Z + mm) * rows_chunk, rows_chunk)],
            rsb.at[p],
            rss.at[k],
            rsr.at[k],
            yz_dev[k],
        )
        for k, (yy, mm) in enumerate(yz_idx)
    ]
    arrive(copies)
    rxb[j] = sum(rsb[k] for k in range(YZ))
    copies = [push(rxb.at[j], rxb.at[j], rxs.at[k], rxr.at[k], dev) for k, dev in enumerate(xc_dev)]
    arrive(copies)
    mine = gfull.at[pl.ds(p * rows_chunk, rows_chunk)]
    gfull[pl.ds(p * rows_chunk, rows_chunk), :] = sum(rxb[k] for k in range(XC))
    copies = [push(mine, mine, ags.at[k], agr.at[k], dev) for k, dev in enumerate(yz_dev)]
    arrive(copies)
    g_out[...] = gfull[...]
    for copy in pending:
        copy.wait_send()


def per_device(dims, flows, routing, tile_block, exp_country, imp_country):
    Y, XC, Z = dims
    YZ = Y * Z
    dma = pltpu.SemaphoreType.DMA
    vmem = functools.partial(pl.BlockSpec, memory_space=pltpu.VMEM)
    smem = functools.partial(pl.BlockSpec, memory_space=pltpu.SMEM)
    cells = SLOTS * SIDE
    pair = (NC, NC)
    sems = []
    for count in ((4, Z - 1), (4, XC - 1), (4, Y - 1), (4, 2), (2, XC - 1), (4, YZ - 1), (YZ - 1,), (XC - 1,), (YZ - 1,)):
        sems += [dma(count), dma(count)]
    a, b, g = pl.pallas_call(
        functools.partial(kernel, dims),
        out_shape=(
            jax.ShapeDtypeStruct((4, NC), F32),
            jax.ShapeDtypeStruct((8, NC), F32),
            jax.ShapeDtypeStruct(pair, F32),
        ),
        in_specs=[smem(), smem(), pl.BlockSpec(memory_space=pl.ANY), vmem(), vmem()],
        out_specs=(vmem(), vmem(), vmem()),
        scratch_shapes=[
            pltpu.VMEM((SLOTS, SIDE, SIDE), BF16),
            pltpu.VMEM((NC, cells), BF16),
            pltpu.VMEM((cells, NC), BF16),
            pltpu.VMEM((SLOTS, 2 * NC, SIDE), BF16),
            pltpu.VMEM((cells, NC), BF16),
            pltpu.VMEM((SLOTS, SIDE, SIDE), F32),
            pltpu.VMEM((SLOTS, SIDE, SIDE), F32),
            pltpu.VMEM((SLOTS, SIDE, SIDE), F32),
            pltpu.VMEM((cells, 2 * NC), BF16),
            pltpu.VMEM((cells, 2 * NC), BF16),
            pltpu.VMEM((8, NC), F32),
            pltpu.VMEM((8, NC), F32),
            pltpu.VMEM(pair, F32),
            pltpu.VMEM(pair, F32),
            pltpu.VMEM(pair, F32),
            pltpu.VMEM(pair, F32),
            pltpu.VMEM(pair, F32),
            pltpu.VMEM((4, Z, 16, NC), F32),
            pltpu.VMEM((4, XC, 16, NC), F32),
            pltpu.VMEM((4, Y, 8, NC), F32),
            pltpu.VMEM((4, 8, NC), F32),
            pltpu.VMEM((4, 2, 8, NC), F32),
            pltpu.VMEM((2, XC, 8, NC), F32),
            pltpu.VMEM((4, YZ, 8, NC), F32),
            pltpu.VMEM((YZ, NC // YZ, NC), F32),
            pltpu.VMEM((XC, NC // YZ, NC), F32),
            pltpu.VMEM(pair, F32),
            dma,
        ]
        + sems,
        compiler_params=pltpu.CompilerParams(collective_id=0, has_side_effects=True),
        name="gravity",
    )(
        routing.reshape(-1),
        tile_block,
        flows,
        exp_country.reshape(4, NC),
        imp_country.reshape(8, NC),
    )
    return a.reshape(-1), b.reshape(-1), g


def solution(mesh, side=8):
    dims = (mesh.shape["exp"] // side, side, mesh.shape["imp"])
    placed = (
        P(("exp", "imp"), None, None),
        P(("exp", "imp"), None, None),
        P(("exp", "imp")),
        P("exp"),
        P("imp"),
    )
    return jax.shard_map(
        functools.partial(per_device, dims),
        mesh=mesh,
        in_specs=placed,
        out_specs=(P("exp"), P("imp"), P()),
        check_vma=False,
    )
```

time: 1650 us -> 82.6 us (0.05)
  blocking collectives: 802 us -> 0 us
  waiting for transfers between devices: 744 us -> 0 us
  Pallas kernels: 0 us -> 78.4 us
  between operations: 38 us -> 0.66 us
  matrix products: 25.8 us -> 0 us
  other arithmetic: 17.9 us -> 0 us
    psum x18 -> x0, blocking collectives: 802 us -> none  [the longest x6 379 us: inner_product(): return lax.psum(local_part(left_vec, right_vec), ('exp', 'imp'))]
    psum x6 -> x0, waiting for transfers between devices: 744 us -> none  [collect(): pair_total = lax.psum(part_pairs, ('exp', 'imp'))]
    pallas_call x0 -> x1, Pallas kernels: none -> 78.4 us  [per_device(): pl.pallas_call(functools.partial(kernel, dims), out_shape=(jax.ShapeDtype...]
    dot_general x36 -> x0, matrix products: 25.8 us -> none  [the longest x6 7.89 us: expand(): jnp.einsum('kim,kjm->kij', row_pairs, col_hot, precision=highest)]
    gather x16 -> x0, local copies, waits for them, and re-layouts: 18.2 us -> none  [the longest x2 6.89 us: per_device(): row_country = exp_country[row_block[:, None] * tile_side + within[None, :]]]
  transfers between devices with their start and end apart: 6 -> 0, of which waited for: 6 -> 0; matrix products, arithmetic and copies ran while one was open for 0% -> 0% of each run, Pallas kernels for 0% -> 0%
where the time goes in v1:
time: 82.6 us; the launch traced here: 82.3 us
  Pallas kernels  78.4 us (95%)
  local copies, waits for them, and re-layouts  3.3 us (4%)
    pallas_call x1, Pallas kernels, per_device(): pl.pallas_call(functools.partial(kernel, dims), out_shape=(jax.ShapeDtype...  78.4 us
    unnamed x7, local copies, waits for them, and re-layouts  3.3 us

profile of v1, /device:TPU:1, one launch (start us, length us, event | category | flops | bytes accessed | tf_op | source)
XLA Modules:
  0.0 82.3 jit_solution(16638265041951066290)
XLA Ops:
  0.6 78.4 %gravity.1 = (f32[4,128]{1,0:T(4,128)}, f32[8,128]{1,0:T(8,128)}, f32[128,128]{1,0:T(8,128)}) custom-call(s32[4]{0:T(128)} %bitcast.9, s32[4]{0:T(128)} %tile_block.1, bf16[4,256,256]{2,1,0:T(8,128)(2,1)} %flows.1, s32[4,128]{1,0:T(4,128)} %bitcast.7, s32[8,128]{1,0:T(8,128)} %bitcast.5), custom_call_target="tpu_custom_call" | custom-call | tf_op jit(solution)/shard_map/gravity/pallas_call | solution.py:424
  79.0 0.0 copy-start.1
  79.0 0.0 copy-start
  79.0 0.7 copy-done.1
  79.7 0.6 copy.11
  80.3 0.0 copy-done
  80.3 0.6 copy.12
  80.9 1.5 %copy.13 = f32[128,128]{1,0:T(8,128)} copy(f32[128,128]{1,0:T(8,128)} %get-tuple-element.14) | data formatting | bytes 131072
Async XLA Ops:
  79.0 0.7 copy-start.1
  79.0 1.2 %copy-start = (f32[8,128]{1,0:T(8,128)S(1)}, f32[8,128]{1,0:T(8,128)}, u32[]{:S(2)}) copy-start(f32[8,128]{1,0:T(8,128)} %get-tuple-element.7) | copy-start | bytes 12292

commit v2 on v1

v2 whole, which is shorter than its diff:
```python
import functools

import jax
import jax.numpy as jnp
from jax import lax
from jax.experimental import pallas as pl
from jax.experimental.pallas import tpu as pltpu
from jax.sharding import PartitionSpec as P

MESH = pl.DeviceIdType.MESH
RIDGE = 64.0
NC = 128
SIDE = 256
SLOTS = 4
F32 = jnp.float32
BF16 = jnp.bfloat16


def split(x):
    hi = x.astype(BF16)
    lo = (x - hi.astype(F32)).astype(BF16)
    return hi, lo


def dot(x, y):
    return lax.dot_general(x, y, (((1,), (0,)), ((), ())), preferred_element_type=F32)


def dot_nt(x, y):
    return lax.dot_general(x, y, (((1,), (1,)), ((), ())), preferred_element_type=F32)


def order(offsets):
    far = lambda off: sum(min(o, 4 - o) for o in off)
    return sorted((off for off in offsets if any(off)), key=far, reverse=True)


def kernel(
    dims,
    routing,
    tile_block,
    flows,
    exp_ids,
    imp_ids,
    a_out,
    b_out,
    g_out,
    fbuf,
    row_t,
    row_s,
    col_t,
    col_s,
    x0,
    xq,
    mu,
    ubuf,
    vbuf,
    va,
    vb,
    r0g,
    qg,
    eg,
    own,
    tabs,
    zb,
    cb,
    yb,
    hs,
    hb,
    cs,
    ps,
    rsb,
    rxb,
    agb,
    fsem,
    z_s,
    z_r,
    c_s,
    c_r,
    y_s,
    y_r,
    h_s,
    h_r,
    cs_s,
    cs_r,
    ps_s,
    ps_r,
    rs_s,
    rs_r,
    rx_s,
    rx_r,
    ag_s,
    ag_r,
):
    Y, XN, Z = dims
    E, XY = 2 * Y * XN, Y * XN
    chunk = NC // XY
    e = lax.axis_index("exp")
    m = lax.axis_index("imp")
    chip = lax.div(e, 2)
    core = lax.rem(e, 2)
    y = lax.div(chip, XN)
    x = lax.rem(chip, XN)
    zc = m * 2 + core

    def device(yy, xx, cc, mm):
        return ((yy * XN + xx) * 2 + cc, mm)

    def step_to(at, off, size):
        return lax.rem(at + off, size) if off else at

    c_dev = [device(y, x, 1 - core, m)]
    z_dev = [(e, lax.rem(m + k, Z)) for k in range(1, Z)]
    xy_at = [
        (step_to(y, oy, Y), step_to(x, ox, XN)) for oy, ox in order([(i, k) for i in range(Y) for k in range(XN)])
    ]
    xy_dev = [device(yy, xx, core, m) for yy, xx in xy_at]
    xyz_dev = [
        device(step_to(y, oy, Y), step_to(x, ox, XN), core, step_to(m, oz, Z))
        for oy, ox, oz in order([(i, k, q) for i in range(Y) for k in range(XN) for q in range(Z)])
    ]
    zc_dev = [
        device(y, x, 1 - core if oc else core, step_to(m, oz, Z))
        for oz, oc in order([(i, k) for i in range(Z) for k in range(2)])
    ]
    after, before = lax.rem(e + 1, E), lax.rem(e + E - 1, E)
    h_dev = [(after, lax.rem(m + k, Z)) for k in range(Z)], [(before, lax.rem(m + k, Z)) for k in range(Z)]
    xy = y * XN + x

    barrier = pltpu.get_barrier_semaphore()
    greet = xy_dev + h_dev[0] + h_dev[1] + zc_dev
    for dev in greet:
        pl.semaphore_signal(barrier, inc=1, device_id=dev, device_id_type=MESH)

    fcopy = pltpu.make_async_copy(flows, fbuf, fsem)
    fcopy.start()

    pending = []

    def push(src, dst, send_sem, recv_sem, dev):
        copy = pltpu.make_async_remote_copy(
            src_ref=src, dst_ref=dst, send_sem=send_sem, recv_sem=recv_sem, device_id=dev, device_id_type=MESH
        )
        copy.start()
        pending.append(copy)
        return copy

    def fan(src, dst, send_sem, recv_sem, devs):
        return [push(src, dst, send_sem.at[k], recv_sem.at[k], dev) for k, dev in enumerate(devs)]

    def arrive(copies):
        for copy in copies:
            copy.wait_recv()

    riota = lax.broadcasted_iota(jnp.int32, (NC, NC), 0)
    ciota = lax.broadcasted_iota(jnp.int32, (NC, NC), 1)
    riota_f, ciota_f = riota.astype(F32), ciota.astype(F32)
    row_blk, col_blk, live = [], [], []
    for k in range(SLOTS):
        blk = tile_block[k]
        row_blk.append(lax.div(blk, 4))
        col_blk.append(lax.rem(blk, 4))
        hit = jnp.int32(0)
        for t in range(routing.shape[0]):
            hit = hit | jnp.where(routing[t] == k, 1, 0)
        live.append(hit)
    erow = [exp_ids[pl.ds(2 * row_blk[k] + h, 1), :] for k in range(SLOTS) for h in range(2)]
    irow = [imp_ids[pl.ds(2 * col_blk[k] + h, 1), :] for k in range(SLOTS) for h in range(2)]
    ids_t = jnp.concatenate(
        [v.astype(F32) for v in erow + irow] + [jnp.zeros((NC - 4 * SLOTS, NC), F32)], axis=0
    ).T
    for q in range(2 * SLOTS):
        k, h = divmod(q, 2)
        row_t[:, NC * q : NC * (q + 1)] = jnp.where(riota == erow[q], 1.0, 0.0).astype(BF16)
        row_s[NC * q : NC * (q + 1), :] = jnp.where(ciota_f == ids_t[:, q : q + 1], 1.0, 0.0).astype(BF16)
        hot = jnp.where(riota == irow[q], 1.0, 0.0).astype(BF16)
        col_t[k, 0:NC, NC * h : NC * (h + 1)] = hot
        col_t[k, NC : 2 * NC, NC * h : NC * (h + 1)] = hot
        col_s[NC * q : NC * (q + 1), :] = jnp.where(
            ciota_f == ids_t[:, 2 * SLOTS + q : 2 * SLOTS + q + 1], 1.0, 0.0
        ).astype(BF16)
    eids, iids = exp_ids[...].astype(F32), imp_ids[...].astype(F32)

    def least(v):
        return jnp.min(jnp.min(v, axis=0, keepdims=True), axis=1, keepdims=True)

    rf = jnp.broadcast_to(least(eids), (1, NC))
    rl = jnp.broadcast_to(-least(-eids), (1, NC))
    cf = jnp.broadcast_to(least(iids), (1, NC))
    cl = jnp.broadcast_to(-least(-iids), (1, NC))
    lane = lax.broadcasted_iota(jnp.int32, (1, NC), 1).astype(F32)
    zero_row = jnp.zeros((1, NC), F32)
    ends = jnp.concatenate(
        [jnp.where(lane == cf, 1.0, 0.0), jnp.where(lane == cl, 1.0, 0.0)] + [zero_row] * 6, axis=0
    ).astype(BF16)
    ones8 = jnp.ones((8, 2 * NC), BF16)
    row_w = [[jnp.where(row_blk[k] == c, 1.0, 0.0) for c in range(2)] for k in range(SLOTS)]
    col_w = [[jnp.where(col_blk[k] == c, 1.0, 0.0) for c in range(4)] for k in range(SLOTS)]

    def keep(k, v):
        return jnp.where(jnp.full(v.shape, live[k]) > 0, v, 0.0)

    def collect(cells):
        sums = []
        for k in range(SLOTS):
            w = cells(k)
            hi, lo = split(w)
            hot = col_s[SIDE * k : SIDE * (k + 1), :]
            vhi, vlo = split(dot(hi, hot) + dot(lo, hot))
            vbuf[SIDE * k : SIDE * (k + 1), 0:NC] = vhi
            vbuf[SIDE * k : SIDE * (k + 1), NC : 2 * NC] = vlo
            sums.append(jnp.sum(w, axis=0, keepdims=True))
        brows = []
        for c in range(4):
            for h in range(2):
                brows.append(sum(col_w[k][c] * sums[k][:, NC * h : NC * (h + 1)] for k in range(SLOTS)))
        return jnp.concatenate(brows, axis=0)

    def b_send(r, bpart):
        cb[r, core] = bpart
        return fan(cb.at[r, core], cb.at[r, core], c_s.at[r], c_r.at[r], c_dev)

    def table_sums():
        v = vbuf[...]
        wide = dot(row_t[...], v)
        table = wide[:, 0:NC] + wide[:, NC : 2 * NC]
        rsum = dot_nt(ones8, v)
        arows = []
        for c in range(2):
            for h in range(2):
                arows.append(
                    sum(
                        row_w[k][c] * rsum[0:1, SIDE * k + NC * h : SIDE * k + NC * (h + 1)]
                        for k in range(SLOTS)
                    )
                )
        return table, arows

    def table_send(r, table, arows):
        first = jnp.sum(jnp.where(riota_f == rf, table, 0.0), axis=0, keepdims=True)
        last = jnp.sum(jnp.where(riota_f == rl, table, 0.0), axis=0, keepdims=True)
        hs[r, 0] = jnp.concatenate([last, rl], axis=0)
        hs[r, 1] = jnp.concatenate([first, rf], axis=0)
        hcopies = []
        for side in range(2):
            hcopies += fan(hs.at[r, side], hb.at[r, side, m], h_s.at[r, side], h_r.at[r, side], h_dev[side])
        hi, lo = split(table)
        edge = dot_nt(ends, jnp.concatenate([hi, lo], axis=0))
        edge = edge[:, 0:NC] + edge[:, NC : 2 * NC]
        zb[r, m] = jnp.concatenate(arows + [edge[0:1], edge[1:2], cf, cl], axis=0)
        zcopies = fan(zb.at[r, m], zb.at[r, m], z_s.at[r], z_r.at[r], z_dev)
        return zcopies, hcopies

    def b_turn(r, ccopies):
        arrive(ccopies)
        yb[r, xy] = cb[r, 0] + cb[r, 1]
        return fan(yb.at[r, xy], yb.at[r, xy], y_s.at[r], y_r.at[r], xy_dev)

    def scal_send(s, rows):
        rows = jnp.sum(jnp.concatenate(rows + [zero_row] * (8 - len(rows)), axis=0), axis=1, keepdims=True)
        cs[s, core] = sum(jnp.where(lane == float(k), rows[k : k + 1], 0.0) for k in range(3))
        return fan(cs.at[s, core], cs.at[s, core], cs_s.at[s], cs_r.at[s], c_dev)

    def scal_turn(s, copies):
        arrive(copies)
        place = xy * Z + m
        ps[s, place] = cs[s, 0] + cs[s, 1]
        return fan(ps.at[s, place], ps.at[s, place], ps_s.at[s], ps_r.at[s], xyz_dev)

    def scal_total(s, copies):
        arrive(copies)
        total = sum(ps[s, k] for k in range(XY * Z))
        return [total[:, k : k + 1] for k in range(3)]

    def columns(r, avec):
        va[0:4, :] = avec
        tiles = [va[pl.ds(2 * row_blk[k] + h, 1), :] for k in range(SLOTS) for h in range(2)]
        prev = zb[r, lax.rem(m + Z - 1, Z), 5:6, :]
        nxt = zb[r, lax.rem(m + 1, Z), 4:5, :]
        return jnp.concatenate(tiles + [prev, nxt, jnp.zeros((NC - 10, NC), F32)], axis=0).T

    def table_end(r, table, cols, hcopies):
        cl_prev = zb[r, lax.rem(m + Z - 1, Z), 7:8, :]
        cf_next = zb[r, lax.rem(m + 1, Z), 6:7, :]
        table = table + jnp.where(ciota_f == cl_prev, cols[:, 8:9], 0.0)
        table = table + jnp.where(ciota_f == cf_next, cols[:, 9:10], 0.0)
        arrive(hcopies)
        from_prev, from_next = (sum(hb[r, side, k] for k in range(Z)) for side in range(2))
        rl_prev, rf_next = hb[r, 0, 0, 1:2, :], hb[r, 1, 0, 1:2, :]
        table = table + jnp.where(riota_f == rl_prev, from_prev[0:1], 0.0)
        table = table + jnp.where(riota_f == rf_next, from_next[0:1], 0.0)
        if r == 0:
            skip_r = jnp.where(rl_prev == rf, 1.0, 0.0)
            skip_c = jnp.where(cl_prev == cf, 1.0, 0.0)
            mine = (riota_f >= rf + skip_r) & (riota_f <= rl) & (ciota_f >= cf + skip_c) & (ciota_f <= cl)
            own[...] = jnp.where(mine, 1.0, 0.0)
        return table

    def b_end(r, ycopies):
        arrive(ycopies)
        return sum(yb[r, k] for k in range(XY))

    def expand(gval, cols, bvec):
        hi, lo = split(gval)
        ubuf[...] = dot(row_s[...], jnp.concatenate([hi, lo], axis=1)).astype(BF16)
        vb[...] = bvec

        def tile(k):
            brow = jnp.concatenate([vb[pl.ds(2 * col_blk[k] + h, 1), :] for h in range(2)], axis=1)
            acol = jnp.concatenate([cols[:, 2 * k + h : 2 * k + h + 1] for h in range(2)], axis=0)
            return dot(ubuf[SIDE * k : SIDE * (k + 1), :], col_t[k]) + acol + brow

        return tile

    def fold(v):
        v = jnp.sum(v.reshape(SIDE // 8, 8, SIDE), axis=0)
        return v[:, 0:NC] + v[:, NC:SIDE]

    def lanes(v):
        return jnp.sum(v, axis=0, keepdims=True)

    def inner(u, v):
        total = lanes(u[0] * v[0]) * (1.0 / Z) + lanes(u[1] * v[1]) * (1.0 / E)
        return total + lanes(own[...] * u[2] * v[2])

    def scatter(lo, hi, part):
        src = tabs.at[pl.ds(lo, hi - lo)]
        rsb[xy, lo:hi] = tabs[lo:hi, pl.ds(xy * chunk, chunk), :]
        return [
            push(
                src.at[:, pl.ds((yy * XN + xx) * chunk, chunk)],
                rsb.at[xy, pl.ds(lo, hi - lo)],
                rs_s.at[part, k],
                rs_r.at[part, k],
                xy_dev[k],
            )
            for k, (yy, xx) in enumerate(xy_at)
        ]

    effects = None
    for newton in range(2):
        final = newton == 1
        r = 2 * newton
        if not final:

            def cells(k):
                mu[k] = keep(k, jnp.ones((SIDE, SIDE), F32))
                return keep(k, fbuf[k].astype(F32) - 1.0)

            fcopy.wait()
        else:

            def cells(k):
                rate = keep(k, jnp.exp(c0 * x0[k] + c1 * (x0[k] - step * xq[k])))
                mu[k] = rate
                return keep(k, fbuf[k].astype(F32)) - rate

        bpart = collect(cells)
        if not final:
            pl.semaphore_wait(barrier, len(greet))
        cc = b_send(r, bpart)
        table, arows = table_sums()
        zcp, hcp = table_send(r, table, arows)
        yc = b_turn(r, cc)
        arrive(zcp)
        ra = sum(zb[r, k, 0:4, :] for k in range(Z))
        if final:
            ra = ra - RIDGE * effects[0]
        cols = columns(r, ra)
        rg = table_end(r, table, cols, hcp)
        if final:
            rg = rg - RIDGE * eg[...]
        rb = b_end(r, yc)
        if final:
            rb = rb - RIDGE * effects[1]
        r0g[...] = rg
        if final:
            tabs[0] = eg[...] * own[...]
            tabs[1] = rg * own[...]
            rs_copies = scatter(0, 2, 0)
        res = (ra, rb, rg)
        tile = expand(rg, cols, rb)
        quad = []

        def cells(k):
            v = tile(k)
            x0[k] = v
            w = mu[k] * v
            quad.append(fold(w * v))
            return w

        bpart = collect(cells)
        sc = scal_send(r, [inner(res, res), lanes(sum(quad))])
        cc = b_send(r + 1, bpart)
        table, arows = table_sums()
        pc = scal_turn(r, sc)
        zcp, hcp = table_send(r + 1, table, arows)
        yc = b_turn(r + 1, cc)
        if final:
            tabs[2] = table
            rs_copies += scatter(2, 3, 1)
        arrive(zcp)
        qa = sum(zb[r + 1, k, 0:4, :] for k in range(Z)) + RIDGE * ra
        cols = columns(r + 1, qa)
        qgv = table_end(r + 1, table, cols, hcp) + RIDGE * r0g[...]
        qg[...] = qgv
        if final:
            arrive(rs_copies)
            rxb[zc] = sum(rsb[k] for k in range(XY))
            rx_copies = fan(rxb.at[zc], rxb.at[zc], rx_s, rx_r, zc_dev)
        qb = b_end(r + 1, yc) + RIDGE * rb
        tile = expand(qgv, cols, qb)
        for k in range(SLOTS):
            xq[k] = tile(k)
        rr, rhr, _ = scal_total(r, pc)
        rhr = rhr + RIDGE * rr
        step = rr / rhr

        quad = []
        for k in range(SLOTS):
            v = x0[k] - step * xq[k]
            quad.append(fold(mu[k] * v * v))
        qvec = (qa, qb, qg[...])
        res1 = (ra - step * qa, rb - step * qb, r0g[...] - step * qg[...])
        sc = scal_send(r + 1, [inner(res1, res1), lanes(sum(quad)), inner(res1, qvec)])
        pc = scal_turn(r + 1, sc)
        if final:
            arrive(rx_copies)
            agb[xy] = sum(rxb[k] for k in range(2 * Z))
            ag_copies = fan(agb.at[xy], agb.at[xy], ag_s, ag_r, xy_dev)
        rr1, curve, cross = scal_total(r + 1, pc)
        beta = rr1 / rr
        curve = curve + RIDGE * rr1 + 2.0 * beta * cross + beta * beta * rhr
        c1 = rr1 / curve
        c0 = step + c1 * beta
        da = c0 * ra + c1 * (ra - step * qa)
        db = c0 * rb + c1 * (rb - step * qb)
        if not final:
            effects = (da, db)
            eg[...] = c0 * r0g[...] + c1 * (r0g[...] - step * qg[...])
        else:
            a_out[...] = effects[0] + da
            b_out[...] = effects[1] + db
            arrive(ag_copies)
            for k in range(XY):
                was, res0, img = agb[k, 0], agb[k, 1], agb[k, 2]
                img = img + RIDGE * res0
                g_out[chunk * k : chunk * (k + 1), :] = was + (c0 * res0 + c1 * (res0 - step * img))
    for copy in pending:
        copy.wait_send()


def per_device(dims, flows, routing, tile_block, exp_country, imp_country):
    Y, XN, Z = dims
    XY = Y * XN
    chunk = NC // XY
    dma = pltpu.SemaphoreType.DMA
    vmem = functools.partial(pl.BlockSpec, memory_space=pltpu.VMEM)
    smem = functools.partial(pl.BlockSpec, memory_space=pltpu.SMEM)
    cells = SLOTS * SIDE
    pair = (NC, NC)
    sems = []
    for count in (
        (4, Z - 1),
        (4, 1),
        (4, XY - 1),
        (4, 2, Z),
        (4, 1),
        (4, XY * Z - 1),
        (2, XY - 1),
        (2 * Z - 1,),
        (XY - 1,),
    ):
        sems += [dma(count), dma(count)]
    a, b, g = pl.pallas_call(
        functools.partial(kernel, dims),
        out_shape=(
            jax.ShapeDtypeStruct((4, NC), F32),
            jax.ShapeDtypeStruct((8, NC), F32),
            jax.ShapeDtypeStruct(pair, F32),
        ),
        in_specs=[smem(), smem(), pl.BlockSpec(memory_space=pl.ANY), vmem(), vmem()],
        out_specs=(vmem(), vmem(), vmem()),
        scratch_shapes=[
            pltpu.VMEM((SLOTS, SIDE, SIDE), BF16),
            pltpu.VMEM((NC, cells), BF16),
            pltpu.VMEM((cells, NC), BF16),
            pltpu.VMEM((SLOTS, 2 * NC, SIDE), BF16),
            pltpu.VMEM((cells, NC), BF16),
            pltpu.VMEM((SLOTS, SIDE, SIDE), F32),
            pltpu.VMEM((SLOTS, SIDE, SIDE), F32),
            pltpu.VMEM((SLOTS, SIDE, SIDE), F32),
            pltpu.VMEM((cells, 2 * NC), BF16),
            pltpu.VMEM((cells, 2 * NC), BF16),
            pltpu.VMEM((8, NC), F32),
            pltpu.VMEM((8, NC), F32),
            pltpu.VMEM(pair, F32),
            pltpu.VMEM(pair, F32),
            pltpu.VMEM(pair, F32),
            pltpu.VMEM(pair, F32),
            pltpu.VMEM((3,) + pair, F32),
            pltpu.VMEM((4, Z, 8, NC), F32),
            pltpu.VMEM((4, 2, 8, NC), F32),
            pltpu.VMEM((4, XY, 8, NC), F32),
            pltpu.VMEM((4, 2, 2, NC), F32),
            pltpu.VMEM((4, 2, Z, 2, NC), F32),
            pltpu.VMEM((4, 2, 1, NC), F32),
            pltpu.VMEM((4, XY * Z, 1, NC), F32),
            pltpu.VMEM((XY, 3, chunk, NC), F32),
            pltpu.VMEM((2 * Z, 3, chunk, NC), F32),
            pltpu.VMEM((XY, 3, chunk, NC), F32),
            dma,
        ]
        + sems,
        compiler_params=pltpu.CompilerParams(collective_id=0, has_side_effects=True),
        name="gravity",
    )(
        routing.reshape(-1),
        tile_block,
        flows,
        exp_country.reshape(4, NC),
        imp_country.reshape(8, NC),
    )
    return a.reshape(-1), b.reshape(-1), g


def solution(mesh, xn=4):
    dims = (mesh.shape["exp"] // (2 * xn), xn, mesh.shape["imp"])
    placed = (
        P(("exp", "imp"), None, None),
        P(("exp", "imp"), None, None),
        P(("exp", "imp")),
        P("exp"),
        P("imp"),
    )
    return jax.shard_map(
        functools.partial(per_device, dims),
        mesh=mesh,
        in_specs=placed,
        out_specs=(P("exp"), P("imp"), P()),
        check_vma=False,
    )
```

time: 82.6 us -> 64.7 us (0.78)
  Pallas kernels: 78.4 us -> 60.4 us
    pallas_call x1, Pallas kernels: 78.4 us -> 60.4 us  [per_device(): pl.pallas_call(functools.partial(kernel, dims), out_shape=(jax.ShapeDtype...]
where the time goes in v2:
time: 64.7 us; the launch traced here: 64.4 us
  Pallas kernels  60.4 us (93%)
  local copies, waits for them, and re-layouts  3.3 us (5%)
  between operations  0.66 us (1%)
    pallas_call x1, Pallas kernels, per_device(): pl.pallas_call(functools.partial(kernel, dims), out_shape=(jax.ShapeDtype...  60.4 us
    unnamed x7, local copies, waits for them, and re-layouts  3.3 us

profile of v2, /device:TPU:1, one launch (start us, length us, event | category | flops | bytes accessed | tf_op | source)
XLA Modules:
  0.0 64.4 jit_solution(546396582667898764)
XLA Ops:
  0.6 60.4 %gravity.1 = (f32[4,128]{1,0:T(4,128)}, f32[8,128]{1,0:T(8,128)}, f32[128,128]{1,0:T(8,128)}) custom-call(s32[4]{0:T(128)} %bitcast.9, s32[4]{0:T(128)} %tile_block.1, bf16[4,256,256]{2,1,0:T(8,128)(2,1)} %flows.1, s32[4,128]{1,0:T(4,128)} %bitcast.7, s32[8,128]{1,0:T(8,128)} %bitcast.5), custom_call_target="tpu_custom_call" | custom-call | tf_op jit(solution)/shard_map/gravity/pallas_call | solution.py:475
  61.1 0.0 copy-start.1
  61.1 0.0 copy-start
  61.1 0.7 %copy-done.1 = f32[4,128]{1,0:T(4,128)S(1)} copy-done((f32[4,128]{1,0:T(4,128)S(1)}, f32[4,128]{1,0:T(4,128)}, u32[]{:S(2)}) %copy-start.1) | copy-done | bytes 2072
  61.8 0.6 copy.11
  62.3 0.0 copy-done
  62.3 0.6 copy.12
  62.9 1.5 %copy.13 = f32[128,128]{1,0:T(8,128)} copy(f32[128,128]{1,0:T(8,128)} %get-tuple-element.14) | data formatting | bytes 131072
Async XLA Ops:
  61.1 0.7 %copy-start.1 = (f32[4,128]{1,0:T(4,128)S(1)}, f32[4,128]{1,0:T(4,128)}, u32[]{:S(2)}) copy-start(f32[4,128]{1,0:T(4,128)} %get-tuple-element.6) | copy-start | bytes 6148
  61.1 1.2 %copy-start = (f32[8,128]{1,0:T(8,128)S(1)}, f32[8,128]{1,0:T(8,128)}, u32[]{:S(2)}) copy-start(f32[8,128]{1,0:T(8,128)} %get-tuple-element.7) | copy-start | bytes 12292

commit v3 on v2

--- a/solution.py
+++ b/solution.py
@@ -63,34 +63,21 @@
     own,
     tabs,
     zb,
-    cb,
-    yb,
+    bb,
     hs,
     hb,
-    cs,
     ps,
     rsb,
     rxb,
     agb,
     fsem,
-    z_s,
-    z_r,
-    c_s,
-    c_r,
-    y_s,
-    y_r,
-    h_s,
-    h_r,
-    cs_s,
-    cs_r,
-    ps_s,
-    ps_r,
-    rs_s,
-    rs_r,
-    rx_s,
-    rx_r,
-    ag_s,
-    ag_r,
+    z_sem,
+    b_sem,
+    h_sem,
+    p_sem,
+    rs_sem,
+    rx_sem,
+    ag_sem,
 ):
     Y, XN, Z = dims
     E, XY = 2 * Y * XN, Y * XN
@@ -109,16 +96,18 @@
     def step_to(at, off, size):
         return lax.rem(at + off, size) if off else at
 
-    c_dev = [device(y, x, 1 - core, m)]
     z_dev = [(e, lax.rem(m + k, Z)) for k in range(1, Z)]
     xy_at = [
         (step_to(y, oy, Y), step_to(x, ox, XN)) for oy, ox in order([(i, k) for i in range(Y) for k in range(XN)])
     ]
     xy_dev = [device(yy, xx, core, m) for yy, xx in xy_at]
-    xyz_dev = [
-        device(step_to(y, oy, Y), step_to(x, ox, XN), core, step_to(m, oz, Z))
-        for oy, ox, oz in order([(i, k, q) for i in range(Y) for k in range(XN) for q in range(Z)])
-    ]
+
+    def shift(oy, ox, oz, oc):
+        return device(step_to(y, oy, Y), step_to(x, ox, XN), 1 - core if oc else core, step_to(m, oz, Z))
+
+    ranges = [(i, k, q, c) for i in range(Y) for k in range(XN) for q in range(Z) for c in range(2)]
+    all_dev = [shift(*off) for off in order(ranges)]
+    plane_dev = [shift(*off) for off in order([off for off in ranges if off[2] == 0])]
     zc_dev = [
         device(y, x, 1 - core if oc else core, step_to(m, oz, Z))
         for oz, oc in order([(i, k) for i in range(Z) for k in range(2)])
@@ -128,29 +117,25 @@
     xy = y * XN + x
 
     barrier = pltpu.get_barrier_semaphore()
-    greet = xy_dev + h_dev[0] + h_dev[1] + zc_dev
+    greet = plane_dev + h_dev[0] + h_dev[1] + zc_dev
     for dev in greet:
         pl.semaphore_signal(barrier, inc=1, device_id=dev, device_id_type=MESH)
 
     fcopy = pltpu.make_async_copy(flows, fbuf, fsem)
     fcopy.start()
 
-    pending = []
-
-    def push(src, dst, send_sem, recv_sem, dev):
-        copy = pltpu.make_async_remote_copy(
-            src_ref=src, dst_ref=dst, send_sem=send_sem, recv_sem=recv_sem, device_id=dev, device_id_type=MESH
-        )
-        copy.start()
-        pending.append(copy)
-        return copy
-
-    def fan(src, dst, send_sem, recv_sem, devs):
-        return [push(src, dst, send_sem.at[k], recv_sem.at[k], dev) for k, dev in enumerate(devs)]
-
-    def arrive(copies):
-        for copy in copies:
-            copy.wait_recv()
+    def push(src, dst, sems, dev):
+        pltpu.make_async_remote_copy(
+            src_ref=src, dst_ref=dst, send_sem=sems.at[0], recv_sem=sems.at[1], device_id=dev, device_id_type=MESH
+        ).start()
+
+    def fan(src, sems, devs):
+        for dev in devs:
+            push(src, src, sems, dev)
+
+    def arrive(whole, sems):
+        for k in (1, 0):
+            pltpu.make_async_copy(whole, whole, sems.at[k]).wait()
 
     riota = lax.broadcasted_iota(jnp.int32, (NC, NC), 0)
     ciota = lax.broadcasted_iota(jnp.int32, (NC, NC), 1)
@@ -217,8 +202,8 @@
         return jnp.concatenate(brows, axis=0)
 
     def b_send(r, bpart):
-        cb[r, core] = bpart
-        return fan(cb.at[r, core], cb.at[r, core], c_s.at[r], c_r.at[r], c_dev)
+        bb[r, e] = bpart
+        fan(bb.at[r, e], b_sem.at[r], plane_dev)
 
     def table_sums():
         v = vbuf[...]
@@ -241,35 +226,24 @@
         last = jnp.sum(jnp.where(riota_f == rl, table, 0.0), axis=0, keepdims=True)
         hs[r, 0] = jnp.concatenate([last, rl], axis=0)
         hs[r, 1] = jnp.concatenate([first, rf], axis=0)
-        hcopies = []
         for side in range(2):
-            hcopies += fan(hs.at[r, side], hb.at[r, side, m], h_s.at[r, side], h_r.at[r, side], h_dev[side])
+            for dev in h_dev[side]:
+                push(hs.at[r, side], hb.at[r, side, m], h_sem.at[r], dev)
         hi, lo = split(table)
         edge = dot_nt(ends, jnp.concatenate([hi, lo], axis=0))
         edge = edge[:, 0:NC] + edge[:, NC : 2 * NC]
         zb[r, m] = jnp.concatenate(arows + [edge[0:1], edge[1:2], cf, cl], axis=0)
-        zcopies = fan(zb.at[r, m], zb.at[r, m], z_s.at[r], z_r.at[r], z_dev)
-        return zcopies, hcopies
-
-    def b_turn(r, ccopies):
-        arrive(ccopies)
-        yb[r, xy] = cb[r, 0] + cb[r, 1]
-        return fan(yb.at[r, xy], yb.at[r, xy], y_s.at[r], y_r.at[r], xy_dev)
+        fan(zb.at[r, m], z_sem.at[r], z_dev)
 
     def scal_send(s, rows):
         rows = jnp.sum(jnp.concatenate(rows + [zero_row] * (8 - len(rows)), axis=0), axis=1, keepdims=True)
-        cs[s, core] = sum(jnp.where(lane == float(k), rows[k : k + 1], 0.0) for k in range(3))
-        return fan(cs.at[s, core], cs.at[s, core], cs_s.at[s], cs_r.at[s], c_dev)
-
-    def scal_turn(s, copies):
-        arrive(copies)
-        place = xy * Z + m
-        ps[s, place] = cs[s, 0] + cs[s, 1]
-        return fan(ps.at[s, place], ps.at[s, place], ps_s.at[s], ps_r.at[s], xyz_dev)
-
-    def scal_total(s, copies):
-        arrive(copies)
-        total = sum(ps[s, k] for k in range(XY * Z))
+        place = e * Z + m
+        ps[s, pl.ds(place, 1), :] = sum(jnp.where(lane == float(k), rows[k : k + 1], 0.0) for k in range(3))
+        fan(ps.at[s, pl.ds(place, 1)], p_sem.at[s], all_dev)
+
+    def scal_total(s):
+        arrive(ps.at[s, pl.ds(0, E * Z - 1)], p_sem.at[s])
+        total = jnp.sum(ps[s], axis=0, keepdims=True)
         return [total[:, k : k + 1] for k in range(3)]
 
     def columns(r, avec):
@@ -279,12 +253,12 @@
         nxt = zb[r, lax.rem(m + 1, Z), 4:5, :]
         return jnp.concatenate(tiles + [prev, nxt, jnp.zeros((NC - 10, NC), F32)], axis=0).T
 
-    def table_end(r, table, cols, hcopies):
+    def table_end(r, table, cols):
         cl_prev = zb[r, lax.rem(m + Z - 1, Z), 7:8, :]
         cf_next = zb[r, lax.rem(m + 1, Z), 6:7, :]
         table = table + jnp.where(ciota_f == cl_prev, cols[:, 8:9], 0.0)
         table = table + jnp.where(ciota_f == cf_next, cols[:, 9:10], 0.0)
-        arrive(hcopies)
+        arrive(hb.at[r], h_sem.at[r])
         from_prev, from_next = (sum(hb[r, side, k] for k in range(Z)) for side in range(2))
         rl_prev, rf_next = hb[r, 0, 0, 1:2, :], hb[r, 1, 0, 1:2, :]
         table = table + jnp.where(riota_f == rl_prev, from_prev[0:1], 0.0)
@@ -296,9 +270,13 @@
             own[...] = jnp.where(mine, 1.0, 0.0)
         return table
 
-    def b_end(r, ycopies):
-        arrive(ycopies)
-        return sum(yb[r, k] for k in range(XY))
+    def z_end(r):
+        arrive(zb.at[r, pl.ds(0, Z - 1)], z_sem.at[r])
+        return sum(zb[r, k, 0:4, :] for k in range(Z))
+
+    def b_end(r):
+        arrive(bb.at[r, pl.ds(0, E - 1)], b_sem.at[r])
+        return sum(bb[r, k] for k in range(E))
 
     def expand(gval, cols, bvec):
         hi, lo = split(gval)
@@ -323,19 +301,11 @@
         total = lanes(u[0] * v[0]) * (1.0 / Z) + lanes(u[1] * v[1]) * (1.0 / E)
         return total + lanes(own[...] * u[2] * v[2])
 
-    def scatter(lo, hi, part):
+    def scatter(lo, hi):
         src = tabs.at[pl.ds(lo, hi - lo)]
         rsb[xy, lo:hi] = tabs[lo:hi, pl.ds(xy * chunk, chunk), :]
-        return [
-            push(
-                src.at[:, pl.ds((yy * XN + xx) * chunk, chunk)],
-                rsb.at[xy, pl.ds(lo, hi - lo)],
-                rs_s.at[part, k],
-                rs_r.at[part, k],
-                xy_dev[k],
-            )
-            for k, (yy, xx) in enumerate(xy_at)
-        ]
+        for (yy, xx), dev in zip(xy_at, xy_dev):
+            push(src.at[:, pl.ds((yy * XN + xx) * chunk, chunk)], rsb.at[xy, pl.ds(lo, hi - lo)], rs_sem, dev)
 
     effects = None
     for newton in range(2):
@@ -358,26 +328,24 @@
         bpart = collect(cells)
         if not final:
             pl.semaphore_wait(barrier, len(greet))
-        cc = b_send(r, bpart)
+        b_send(r, bpart)
         table, arows = table_sums()
-        zcp, hcp = table_send(r, table, arows)
-        yc = b_turn(r, cc)
-        arrive(zcp)
-        ra = sum(zb[r, k, 0:4, :] for k in range(Z))
+        table_send(r, table, arows)
+        ra = z_end(r)
         if final:
             ra = ra - RIDGE * effects[0]
         cols = columns(r, ra)
-        rg = table_end(r, table, cols, hcp)
+        rg = table_end(r, table, cols)
         if final:
             rg = rg - RIDGE * eg[...]
-        rb = b_end(r, yc)
+        rb = b_end(r)
         if final:
             rb = rb - RIDGE * effects[1]
         r0g[...] = rg
         if final:
             tabs[0] = eg[...] * own[...]
             tabs[1] = rg * own[...]
-            rs_copies = scatter(0, 2, 0)
+            scatter(0, 2)
         res = (ra, rb, rg)
         tile = expand(rg, cols, rb)
         quad = []
@@ -390,29 +358,26 @@
             return w
 
         bpart = collect(cells)
-        sc = scal_send(r, [inner(res, res), lanes(sum(quad))])
-        cc = b_send(r + 1, bpart)
+        scal_send(r, [inner(res, res), lanes(sum(quad))])
+        b_send(r + 1, bpart)
         table, arows = table_sums()
-        pc = scal_turn(r, sc)
-        zcp, hcp = table_send(r + 1, table, arows)
-        yc = b_turn(r + 1, cc)
+        table_send(r + 1, table, arows)
         if final:
             tabs[2] = table
-            rs_copies += scatter(2, 3, 1)
-        arrive(zcp)
-        qa = sum(zb[r + 1, k, 0:4, :] for k in range(Z)) + RIDGE * ra
+            scatter(2, 3)
+        qa = z_end(r + 1) + RIDGE * ra
         cols = columns(r + 1, qa)
-        qgv = table_end(r + 1, table, cols, hcp) + RIDGE * r0g[...]
+        qgv = table_end(r + 1, table, cols) + RIDGE * r0g[...]
         qg[...] = qgv
         if final:
-            arrive(rs_copies)
+            arrive(rsb.at[pl.ds(0, XY - 1)], rs_sem)
             rxb[zc] = sum(rsb[k] for k in range(XY))
-            rx_copies = fan(rxb.at[zc], rxb.at[zc], rx_s, rx_r, zc_dev)
-        qb = b_end(r + 1, yc) + RIDGE * rb
+            fan(rxb.at[zc], rx_sem, zc_dev)
+        qb = b_end(r + 1) + RIDGE * rb
         tile = expand(qgv, cols, qb)
         for k in range(SLOTS):
             xq[k] = tile(k)
-        rr, rhr, _ = scal_total(r, pc)
+        rr, rhr, _ = scal_total(r)
         rhr = rhr + RIDGE * rr
         step = rr / rhr
 
@@ -422,13 +387,12 @@
             quad.append(fold(mu[k] * v * v))
         qvec = (qa, qb, qg[...])
         res1 = (ra - step * qa, rb - step * qb, r0g[...] - step * qg[...])
-        sc = scal_send(r + 1, [inner(res1, res1), lanes(sum(quad)), inner(res1, qvec)])
-        pc = scal_turn(r + 1, sc)
-        if final:
-            arrive(rx_copies)
+        scal_send(r + 1, [inner(res1, res1), lanes(sum(quad)), inner(res1, qvec)])
+        if final:
+            arrive(rxb.at[pl.ds(0, 2 * Z - 1)], rx_sem)
             agb[xy] = sum(rxb[k] for k in range(2 * Z))
-            ag_copies = fan(agb.at[xy], agb.at[xy], ag_s, ag_r, xy_dev)
-        rr1, curve, cross = scal_total(r + 1, pc)
+            fan(agb.at[xy], ag_sem, xy_dev)
+        rr1, curve, cross = scal_total(r + 1)
         beta = rr1 / rr
         curve = curve + RIDGE * rr1 + 2.0 * beta * cross + beta * beta * rhr
         c1 = rr1 / curve
@@ -441,14 +405,11 @@
         else:
             a_out[...] = effects[0] + da
             b_out[...] = effects[1] + db
-            arrive(ag_copies)
+            arrive(agb.at[pl.ds(0, XY - 1)], ag_sem)
             for k in range(XY):
                 was, res0, img = agb[k, 0], agb[k, 1], agb[k, 2]
                 img = img + RIDGE * res0
                 g_out[chunk * k : chunk * (k + 1), :] = was + (c0 * res0 + c1 * (res0 - step * img))
-    for copy in pending:
-        copy.wait_send()
-
 
 def per_device(dims, flows, routing, tile_block, exp_country, imp_country):
     Y, XN, Z = dims
@@ -459,19 +420,7 @@
     smem = functools.partial(pl.BlockSpec, memory_space=pltpu.SMEM)
     cells = SLOTS * SIDE
     pair = (NC, NC)
-    sems = []
-    for count in (
-        (4, Z - 1),
-        (4, 1),
-        (4, XY - 1),
-        (4, 2, Z),
-        (4, 1),
-        (4, XY * Z - 1),
-        (2, XY - 1),
-        (2 * Z - 1,),
-        (XY - 1,),
-    ):
-        sems += [dma(count), dma(count)]
+    sems = [dma((4, 2))] * 4 + [dma((2,))] * 3
     a, b, g = pl.pallas_call(
         functools.partial(kernel, dims),
         out_shape=(
@@ -500,12 +449,10 @@
             pltpu.VMEM(pair, F32),
             pltpu.VMEM((3,) + pair, F32),
             pltpu.VMEM((4, Z, 8, NC), F32),
-            pltpu.VMEM((4, 2, 8, NC), F32),
-            pltpu.VMEM((4, XY, 8, NC), F32),
+            pltpu.VMEM((4, 2 * XY, 8, NC), F32),
             pltpu.VMEM((4, 2, 2, NC), F32),
             pltpu.VMEM((4, 2, Z, 2, NC), F32),
-            pltpu.VMEM((4, 2, 1, NC), F32),
-            pltpu.VMEM((4, XY * Z, 1, NC), F32),
+            pltpu.VMEM((4, 2 * XY * Z, NC), F32),
             pltpu.VMEM((XY, 3, chunk, NC), F32),
             pltpu.VMEM((2 * Z, 3, chunk, NC), F32),
             pltpu.VMEM((XY, 3, chunk, NC), F32),

time: 64.7 us -> 57.9 us (0.89)
  Pallas kernels: 60.4 us -> 53.6 us
    pallas_call x1, Pallas kernels: 60.4 us -> 53.6 us  [per_device(): pl.pallas_call(functools.partial(kernel, dims), out_shape=(jax.ShapeDtype...]
where the time goes in v3:
time: 57.9 us; the launch traced here: 57.6 us
  Pallas kernels  53.6 us (93%)
  local copies, waits for them, and re-layouts  3.3 us (6%)
  between operations  0.66 us (1%)
    pallas_call x1, Pallas kernels, per_device(): pl.pallas_call(functools.partial(kernel, dims), out_shape=(jax.ShapeDtype...  53.6 us
    unnamed x7, local copies, waits for them, and re-layouts  3.3 us

profile of v3, /device:TPU:1, one launch (start us, length us, event | category | flops | bytes accessed | tf_op | source)
XLA Modules:
  0.0 57.6 jit_solution(7730005231924997266)
XLA Ops:
  0.6 53.6 %gravity.1 = (f32[4,128]{1,0:T(4,128)}, f32[8,128]{1,0:T(8,128)}, f32[128,128]{1,0:T(8,128)}) custom-call(s32[4]{0:T(128)} %bitcast.9, s32[4]{0:T(128)} %tile_block.1, bf16[4,256,256]{2,1,0:T(8,128)(2,1)} %flows.1, s32[4,128]{1,0:T(4,128)} %bitcast.7, s32[8,128]{1,0:T(8,128)} %bitcast.5), custom_call_target="tpu_custom_call" | custom-call | tf_op jit(solution)/shard_map/gravity/pallas_call | solution.py:424
  54.2 0.0 copy-start.1
  54.2 0.0 copy-start
  54.3 0.7 %copy-done.1 = f32[4,128]{1,0:T(4,128)S(1)} copy-done((f32[4,128]{1,0:T(4,128)S(1)}, f32[4,128]{1,0:T(4,128)}, u32[]{:S(2)}) %copy-start.1) | copy-done | bytes 2072
  54.9 0.6 %copy.11 = f32[512]{0:T(512)} copy(f32[512]{0:T(512)S(1)} %bitcast.8) | data formatting | bytes 4096
  55.5 0.0 copy-done
  55.5 0.6 %copy.12 = f32[1024]{0:T(1024)} copy(f32[1024]{0:T(1024)S(1)} %bitcast.6) | data formatting | bytes 8192
  56.1 1.5 %copy.13 = f32[128,128]{1,0:T(8,128)} copy(f32[128,128]{1,0:T(8,128)} %get-tuple-element.14) | data formatting | bytes 131072
Async XLA Ops:
  54.2 0.7 %copy-start.1 = (f32[4,128]{1,0:T(4,128)S(1)}, f32[4,128]{1,0:T(4,128)}, u32[]{:S(2)}) copy-start(f32[4,128]{1,0:T(4,128)} %get-tuple-element.6) | copy-start | bytes 6148
  54.2 1.2 %copy-start = (f32[8,128]{1,0:T(8,128)S(1)}, f32[8,128]{1,0:T(8,128)}, u32[]{:S(2)}) copy-start(f32[8,128]{1,0:T(8,128)} %get-tuple-element.7) | copy-start | bytes 12292

commit v4 on v3

--- a/solution.py
+++ b/solution.py
@@ -30,9 +30,12 @@
     return lax.dot_general(x, y, (((1,), (1,)), ((), ())), preferred_element_type=F32)
 
 
+def hops(off):
+    return sum(min(o, 4 - o) for o in off[:3])
+
+
 def order(offsets):
-    far = lambda off: sum(min(o, 4 - o) for o in off)
-    return sorted((off for off in offsets if any(off)), key=far, reverse=True)
+    return sorted((off for off in offsets if any(off)), key=hops, reverse=True)
 
 
 def kernel(
@@ -54,6 +57,7 @@
     xq,
     mu,
     ubuf,
+    wbuf,
     vbuf,
     va,
     vb,
@@ -62,6 +66,9 @@
     eg,
     own,
     tabs,
+    image,
+    parts,
+    gathered,
     zb,
     bb,
     hs,
@@ -78,6 +85,8 @@
     rs_sem,
     rx_sem,
     ag_sem,
+    part_sem,
+    gath_sem,
 ):
     Y, XN, Z = dims
     E, XY = 2 * Y * XN, Y * XN
@@ -106,7 +115,12 @@
         return device(step_to(y, oy, Y), step_to(x, ox, XN), 1 - core if oc else core, step_to(m, oz, Z))
 
     ranges = [(i, k, q, c) for i in range(Y) for k in range(XN) for q in range(Z) for c in range(2)]
-    all_dev = [shift(*off) for off in order(ranges)]
+    far_dev = [shift(*off) for off in order(ranges) if hops(off) >= 5]
+    mid_dev = [shift(*off) for off in order(ranges) if hops(off) == 4]
+    near_dev = [shift(*off) for off in order(ranges) if hops(off) <= 3]
+    all_dev = far_dev + mid_dev + near_dev
+    me = e * Z + m
+    own_rows = NC // (E * Z)
     plane_dev = [shift(*off) for off in order([off for off in ranges if off[2] == 0])]
     zc_dev = [
         device(y, x, 1 - core if oc else core, step_to(m, oz, Z))
@@ -190,10 +204,8 @@
         for k in range(SLOTS):
             w = cells(k)
             hi, lo = split(w)
-            hot = col_s[SIDE * k : SIDE * (k + 1), :]
-            vhi, vlo = split(dot(hi, hot) + dot(lo, hot))
-            vbuf[SIDE * k : SIDE * (k + 1), 0:NC] = vhi
-            vbuf[SIDE * k : SIDE * (k + 1), NC : 2 * NC] = vlo
+            wbuf[k, :, 0:SIDE] = hi
+            wbuf[k, :, SIDE : 2 * SIDE] = lo
             sums.append(jnp.sum(w, axis=0, keepdims=True))
         brows = []
         for c in range(4):
@@ -206,6 +218,11 @@
         fan(bb.at[r, e], b_sem.at[r], plane_dev)
 
     def table_sums():
+        for k in range(SLOTS):
+            hot = col_s[SIDE * k : SIDE * (k + 1), :]
+            vhi, vlo = split(dot(wbuf[k, :, 0:SIDE], hot) + dot(wbuf[k, :, SIDE : 2 * SIDE], hot))
+            vbuf[SIDE * k : SIDE * (k + 1), 0:NC] = vhi
+            vbuf[SIDE * k : SIDE * (k + 1), NC : 2 * NC] = vlo
         v = vbuf[...]
         wide = dot(row_t[...], v)
         table = wide[:, 0:NC] + wide[:, NC : 2 * NC]
@@ -235,11 +252,12 @@
         zb[r, m] = jnp.concatenate(arows + [edge[0:1], edge[1:2], cf, cl], axis=0)
         fan(zb.at[r, m], z_sem.at[r], z_dev)
 
-    def scal_send(s, rows):
+    def scal_store(s, rows):
         rows = jnp.sum(jnp.concatenate(rows + [zero_row] * (8 - len(rows)), axis=0), axis=1, keepdims=True)
-        place = e * Z + m
-        ps[s, pl.ds(place, 1), :] = sum(jnp.where(lane == float(k), rows[k : k + 1], 0.0) for k in range(3))
-        fan(ps.at[s, pl.ds(place, 1)], p_sem.at[s], all_dev)
+        ps[s, pl.ds(me, 1), :] = sum(jnp.where(lane == float(k), rows[k : k + 1], 0.0) for k in range(3))
+
+    def scal_fan(s, devs):
+        fan(ps.at[s, pl.ds(me, 1)], p_sem.at[s], devs)
 
     def scal_total(s):
         arrive(ps.at[s, pl.ds(0, E * Z - 1)], p_sem.at[s])
@@ -278,9 +296,11 @@
         arrive(bb.at[r, pl.ds(0, E - 1)], b_sem.at[r])
         return sum(bb[r, k] for k in range(E))
 
-    def expand(gval, cols, bvec):
+    def select(gval):
         hi, lo = split(gval)
         ubuf[...] = dot(row_s[...], jnp.concatenate([hi, lo], axis=1)).astype(BF16)
+
+    def expand(cols, bvec):
         vb[...] = bvec
 
         def tile(k):
@@ -301,11 +321,23 @@
         total = lanes(u[0] * v[0]) * (1.0 / Z) + lanes(u[1] * v[1]) * (1.0 / E)
         return total + lanes(own[...] * u[2] * v[2])
 
-    def scatter(lo, hi):
-        src = tabs.at[pl.ds(lo, hi - lo)]
-        rsb[xy, lo:hi] = tabs[lo:hi, pl.ds(xy * chunk, chunk), :]
+    def scatter():
+        rsb[xy] = tabs[:, pl.ds(xy * chunk, chunk), :]
         for (yy, xx), dev in zip(xy_at, xy_dev):
-            push(src.at[:, pl.ds((yy * XN + xx) * chunk, chunk)], rsb.at[xy, pl.ds(lo, hi - lo)], rs_sem, dev)
+            push(tabs.at[:, pl.ds((yy * XN + xx) * chunk, chunk)], rsb.at[xy], rs_sem, dev)
+
+    def rows_out():
+        parts[pl.ds(me * own_rows, own_rows), :] = image[pl.ds(me * own_rows, own_rows), :]
+        for ee, mm in all_dev:
+            src = image.at[pl.ds((ee * Z + mm) * own_rows, own_rows)]
+            push(src, parts.at[pl.ds(me * own_rows, own_rows)], part_sem, (ee, mm))
+
+    def rows_back():
+        arrive(parts.at[pl.ds(0, NC - own_rows)], part_sem)
+        gathered[pl.ds(me * own_rows, own_rows), :] = jnp.sum(
+            parts[...].reshape(E * Z, own_rows, NC), axis=0
+        ) if own_rows > 1 else jnp.sum(parts[...], axis=0, keepdims=True)
+        fan(gathered.at[pl.ds(me * own_rows, own_rows)], gath_sem, all_dev)
 
     effects = None
     for newton in range(2):
@@ -331,6 +363,10 @@
         b_send(r, bpart)
         table, arows = table_sums()
         table_send(r, table, arows)
+        if final:
+            tabs[0] = eg[...] * own[...]
+            tabs[1] = table
+            scatter()
         ra = z_end(r)
         if final:
             ra = ra - RIDGE * effects[0]
@@ -338,16 +374,13 @@
         rg = table_end(r, table, cols)
         if final:
             rg = rg - RIDGE * eg[...]
+        r0g[...] = rg
+        select(rg)
         rb = b_end(r)
         if final:
             rb = rb - RIDGE * effects[1]
-        r0g[...] = rg
-        if final:
-            tabs[0] = eg[...] * own[...]
-            tabs[1] = rg * own[...]
-            scatter(0, 2)
         res = (ra, rb, rg)
-        tile = expand(rg, cols, rb)
+        tile = expand(cols, rb)
         quad = []
 
         def cells(k):
@@ -358,23 +391,26 @@
             return w
 
         bpart = collect(cells)
-        scal_send(r, [inner(res, res), lanes(sum(quad))])
+        scal_store(r, [inner(res, res), lanes(sum(quad))])
+        scal_fan(r, far_dev)
         b_send(r + 1, bpart)
+        scal_fan(r, mid_dev)
         table, arows = table_sums()
         table_send(r + 1, table, arows)
+        scal_fan(r, near_dev)
         if final:
-            tabs[2] = table
-            scatter(2, 3)
+            arrive(rsb.at[pl.ds(0, XY - 1)], rs_sem)
+            rxb[zc] = sum(rsb[k] for k in range(XY))
+            fan(rxb.at[zc], rx_sem, zc_dev)
+            image[...] = table
+            rows_out()
         qa = z_end(r + 1) + RIDGE * ra
         cols = columns(r + 1, qa)
         qgv = table_end(r + 1, table, cols) + RIDGE * r0g[...]
         qg[...] = qgv
-        if final:
-            arrive(rsb.at[pl.ds(0, XY - 1)], rs_sem)
-            rxb[zc] = sum(rsb[k] for k in range(XY))
-            fan(rxb.at[zc], rx_sem, zc_dev)
+        select(qgv)
         qb = b_end(r + 1) + RIDGE * rb
-        tile = expand(qgv, cols, qb)
+        tile = expand(cols, qb)
         for k in range(SLOTS):
             xq[k] = tile(k)
         rr, rhr, _ = scal_total(r)
@@ -387,8 +423,10 @@
             quad.append(fold(mu[k] * v * v))
         qvec = (qa, qb, qg[...])
         res1 = (ra - step * qa, rb - step * qb, r0g[...] - step * qg[...])
-        scal_send(r + 1, [inner(res1, res1), lanes(sum(quad)), inner(res1, qvec)])
+        scal_store(r + 1, [inner(res1, res1), lanes(sum(quad)), inner(res1, qvec)])
+        scal_fan(r + 1, all_dev)
         if final:
+            rows_back()
             arrive(rxb.at[pl.ds(0, 2 * Z - 1)], rx_sem)
             agb[xy] = sum(rxb[k] for k in range(2 * Z))
             fan(agb.at[xy], ag_sem, xy_dev)
@@ -406,10 +444,18 @@
             a_out[...] = effects[0] + da
             b_out[...] = effects[1] + db
             arrive(agb.at[pl.ds(0, XY - 1)], ag_sem)
+            arrive(gathered.at[pl.ds(0, NC - own_rows)], gath_sem)
             for k in range(XY):
-                was, res0, img = agb[k, 0], agb[k, 1], agb[k, 2]
-                img = img + RIDGE * res0
+                was = agb[k, 0]
+                res0 = agb[k, 1] - RIDGE * was
+                img = gathered[chunk * k : chunk * (k + 1), :] + RIDGE * res0
                 g_out[chunk * k : chunk * (k + 1), :] = was + (c0 * res0 + c1 * (res0 - step * img))
+
+def publish(a, b, g, a_out, b_out, g_out):
+    a_out[...] = a[...]
+    b_out[...] = b[...]
+    g_out[...] = g[...]
+
 
 def per_device(dims, flows, routing, tile_block, exp_country, imp_country):
     Y, XN, Z = dims
@@ -420,7 +466,7 @@
     smem = functools.partial(pl.BlockSpec, memory_space=pltpu.SMEM)
     cells = SLOTS * SIDE
     pair = (NC, NC)
-    sems = [dma((4, 2))] * 4 + [dma((2,))] * 3
+    sems = [dma((4, 2))] * 4 + [dma((2,))] * 5
     a, b, g = pl.pallas_call(
         functools.partial(kernel, dims),
         out_shape=(
@@ -440,6 +486,7 @@
             pltpu.VMEM((SLOTS, SIDE, SIDE), F32),
             pltpu.VMEM((SLOTS, SIDE, SIDE), F32),
             pltpu.VMEM((cells, 2 * NC), BF16),
+            pltpu.VMEM((SLOTS, SIDE, 2 * SIDE), BF16),
             pltpu.VMEM((cells, 2 * NC), BF16),
             pltpu.VMEM((8, NC), F32),
             pltpu.VMEM((8, NC), F32),
@@ -447,15 +494,18 @@
             pltpu.VMEM(pair, F32),
             pltpu.VMEM(pair, F32),
             pltpu.VMEM(pair, F32),
-            pltpu.VMEM((3,) + pair, F32),
+            pltpu.VMEM((2,) + pair, F32),
+            pltpu.VMEM(pair, F32),
+            pltpu.VMEM(pair, F32),
+            pltpu.VMEM(pair, F32),
             pltpu.VMEM((4, Z, 8, NC), F32),
             pltpu.VMEM((4, 2 * XY, 8, NC), F32),
             pltpu.VMEM((4, 2, 2, NC), F32),
             pltpu.VMEM((4, 2, Z, 2, NC), F32),
             pltpu.VMEM((4, 2 * XY * Z, NC), F32),
-            pltpu.VMEM((XY, 3, chunk, NC), F32),
-            pltpu.VMEM((2 * Z, 3, chunk, NC), F32),
-            pltpu.VMEM((XY, 3, chunk, NC), F32),
+            pltpu.VMEM((XY, 2, chunk, NC), F32),
+            pltpu.VMEM((2 * Z, 2, chunk, NC), F32),
+            pltpu.VMEM((XY, 2, chunk, NC), F32),
             dma,
         ]
         + sems,
@@ -468,6 +518,17 @@
         exp_country.reshape(4, NC),
         imp_country.reshape(8, NC),
     )
+    a, b, g = pl.pallas_call(
+        publish,
+        out_shape=(
+            jax.ShapeDtypeStruct((4, NC), F32),
+            jax.ShapeDtypeStruct((8, NC), F32),
+            jax.ShapeDtypeStruct(pair, F32),
+        ),
+        in_specs=[vmem()] * 3,
+        out_specs=(vmem(), vmem(), vmem()),
+        name="publish",
+    )(a, b, g)
     return a.reshape(-1), b.reshape(-1), g
 
 

time: 57.9 us -> 54.5 us (0.941)
  local copies, waits for them, and re-layouts: 3.3 us -> 0 us
    unnamed x7 -> x0, local copies, waits for them, and re-layouts: 3.3 us -> none
    pallas_call x0 -> x1, Pallas kernels: none -> 1.49 us  [per_device(): pl.pallas_call(publish, out_shape=(jax.ShapeDtypeStruct((4, NC), F32), ja...]
    pallas_call x1, Pallas kernels: 53.6 us -> 52.1 us  [per_device(): pl.pallas_call(functools.partial(kernel, dims), out_shape=(jax.ShapeDtype...]
where the time goes in v4:
time: 54.5 us; the launch traced here: 54.2 us
  Pallas kernels  53.6 us (98%)
  between operations  0.64 us (1%)
    pallas_call x1, Pallas kernels, per_device(): pl.pallas_call(functools.partial(kernel, dims), out_shape=(jax.ShapeDtype...  52.1 us
    pallas_call x1, Pallas kernels, per_device(): pl.pallas_call(publish, out_shape=(jax.ShapeDtypeStruct((4, NC), F32), ja...  1.49 us

profile of v4, /device:TPU:1, one launch (start us, length us, event | category | flops | bytes accessed | tf_op | source)
XLA Modules:
  0.0 54.2 jit_solution(4244056542388006567)
XLA Ops:
  0.6 52.1 %gravity.1 = (f32[4,128]{1,0:T(4,128)}, f32[8,128]{1,0:T(8,128)}, f32[128,128]{1,0:T(8,128)}) custom-call(s32[4]{0:T(128)} %bitcast.7, s32[4]{0:T(128)} %tile_block.1, bf16[4,256,256]{2,1,0:T(8,128)(2,1)} %flows.1, s32[4,128]{1,0:T(4,128)} %bitcast.6, s32[8,128]{1,0:T(8,128)} %bitcast.5), custom_call_target="tpu_custom_call" | custom-call | tf_op jit(solution)/shard_map/gravity/pallas_call | solution.py:470
  52.8 1.5 %publish.1 = (f32[4,128]{1,0:T(4,128)}, f32[8,128]{1,0:T(8,128)}, f32[128,128]{1,0:T(8,128)}) custom-call(f32[4,128]{1,0:T(4,128)} %get-tuple-element.9.a, f32[8,128]{1,0:T(8,128)} %get-tuple-element.10.b, f32[128,128]{1,0:T(8,128)} %get-tuple-element.11.g), custom_call_target="tpu_custom_call" | custom-call | tf_op jit(solution)/shard_map/publish/pallas_call | solution.py:521

commit v5 on v4

--- a/solution.py
+++ b/solution.py
@@ -213,8 +213,10 @@
                 brows.append(sum(col_w[k][c] * sums[k][:, NC * h : NC * (h + 1)] for k in range(SLOTS)))
         return jnp.concatenate(brows, axis=0)
 
-    def b_send(r, bpart):
+    def b_store(r, bpart):
         bb[r, e] = bpart
+
+    def b_send(r):
         fan(bb.at[r, e], b_sem.at[r], plane_dev)
 
     def table_sums():
@@ -238,19 +240,31 @@
                 )
         return table, arows
 
-    def table_send(r, table, arows):
+    def table_store(r, table, arows):
         first = jnp.sum(jnp.where(riota_f == rf, table, 0.0), axis=0, keepdims=True)
         last = jnp.sum(jnp.where(riota_f == rl, table, 0.0), axis=0, keepdims=True)
         hs[r, 0] = jnp.concatenate([last, rl], axis=0)
         hs[r, 1] = jnp.concatenate([first, rf], axis=0)
+
+    def rows_send(r):
         for side in range(2):
             for dev in h_dev[side]:
                 push(hs.at[r, side], hb.at[r, side, m], h_sem.at[r], dev)
+
+    def edge_store(r, table, arows):
         hi, lo = split(table)
         edge = dot_nt(ends, jnp.concatenate([hi, lo], axis=0))
         edge = edge[:, 0:NC] + edge[:, NC : 2 * NC]
         zb[r, m] = jnp.concatenate(arows + [edge[0:1], edge[1:2], cf, cl], axis=0)
+
+    def edge_send(r):
         fan(zb.at[r, m], z_sem.at[r], z_dev)
+
+    def table_send(r, table, arows):
+        table_store(r, table, arows)
+        rows_send(r)
+        edge_store(r, table, arows)
+        edge_send(r)
 
     def scal_store(s, rows):
         rows = jnp.sum(jnp.concatenate(rows + [zero_row] * (8 - len(rows)), axis=0), axis=1, keepdims=True)
@@ -358,11 +372,19 @@
                 return keep(k, fbuf[k].astype(F32)) - rate
 
         bpart = collect(cells)
+        b_store(r, bpart)
         if not final:
+            table, arows = table_sums()
+            table_store(r, table, arows)
+            edge_store(r, table, arows)
             pl.semaphore_wait(barrier, len(greet))
-        b_send(r, bpart)
-        table, arows = table_sums()
-        table_send(r, table, arows)
+            b_send(r)
+            rows_send(r)
+            edge_send(r)
+        else:
+            b_send(r)
+            table, arows = table_sums()
+            table_send(r, table, arows)
         if final:
             tabs[0] = eg[...] * own[...]
             tabs[1] = table
@@ -393,7 +415,8 @@
         bpart = collect(cells)
         scal_store(r, [inner(res, res), lanes(sum(quad))])
         scal_fan(r, far_dev)
-        b_send(r + 1, bpart)
+        b_store(r + 1, bpart)
+        b_send(r + 1)
         scal_fan(r, mid_dev)
         table, arows = table_sums()
         table_send(r + 1, table, arows)
@@ -451,10 +474,12 @@
                 img = gathered[chunk * k : chunk * (k + 1), :] + RIDGE * res0
                 g_out[chunk * k : chunk * (k + 1), :] = was + (c0 * res0 + c1 * (res0 - step * img))
 
-def publish(a, b, g, a_out, b_out, g_out):
-    a_out[...] = a[...]
-    b_out[...] = b[...]
-    g_out[...] = g[...]
+def publish(a, b, g, a_out, b_out, g_out, sems):
+    copies = [pltpu.make_async_copy(src, dst, sems.at[k]) for k, (src, dst) in enumerate(((g, g_out), (a, a_out), (b, b_out)))]
+    for copy in copies:
+        copy.start()
+    for copy in copies:
+        copy.wait()
 
 
 def per_device(dims, flows, routing, tile_block, exp_country, imp_country):
@@ -469,11 +494,7 @@
     sems = [dma((4, 2))] * 4 + [dma((2,))] * 5
     a, b, g = pl.pallas_call(
         functools.partial(kernel, dims),
-        out_shape=(
-            jax.ShapeDtypeStruct((4, NC), F32),
-            jax.ShapeDtypeStruct((8, NC), F32),
-            jax.ShapeDtypeStruct(pair, F32),
-        ),
+        out_shape=(pltpu.VMEM((4, NC), F32), pltpu.VMEM((8, NC), F32), pltpu.VMEM(pair, F32)),
         in_specs=[smem(), smem(), pl.BlockSpec(memory_space=pl.ANY), vmem(), vmem()],
         out_specs=(vmem(), vmem(), vmem()),
         scratch_shapes=[
@@ -525,10 +546,11 @@
             jax.ShapeDtypeStruct((8, NC), F32),
             jax.ShapeDtypeStruct(pair, F32),
         ),
-        in_specs=[vmem()] * 3,
-        out_specs=(vmem(), vmem(), vmem()),
+        in_specs=[pl.BlockSpec(memory_space=pl.ANY)] * 3,
+        out_specs=(pl.BlockSpec(memory_space=pl.ANY),) * 3,
+        scratch_shapes=[pltpu.SemaphoreType.DMA((3,))],
         name="publish",
-    )(a, b, g)
+    )(*(pltpu.with_memory_space_constraint(v, pltpu.VMEM) for v in (a, b, g)))
     return a.reshape(-1), b.reshape(-1), g
 
 

time: 54.5 us -> 52.9 us (0.971)
  Pallas kernels: 53.6 us -> 52.1 us
    pallas_call x1, Pallas kernels: 1.49 us -> 0.66 us  [per_device(): pl.pallas_call(publish, out_shape=(jax.ShapeDtypeStruct((4, NC), F32), ja...]
    pallas_call x1, Pallas kernels: 52.1 us -> 51.4 us  [per_device(): pl.pallas_call(functools.partial(kernel, dims), out_shape=(pltpu.VMEM((4,...]
where the time goes in v5:
time: 52.9 us; the launch traced here: 52.7 us
  Pallas kernels  52.1 us (98%)
  between operations  0.64 us (1%)
    pallas_call x1, Pallas kernels, per_device(): pl.pallas_call(functools.partial(kernel, dims), out_shape=(pltpu.VMEM((4,...  51.4 us

profile of v5, /device:TPU:1, one launch (start us, length us, event | category | flops | bytes accessed | tf_op | source)
XLA Modules:
  0.0 52.7 jit_solution(5246441748056456609)
XLA Ops:
  0.6 51.4 %gravity.1 = (f32[4,128]{1,0:T(4,128)S(1)}, f32[8,128]{1,0:T(8,128)S(1)}, f32[128,128]{1,0:T(8,128)S(1)}) custom-call(s32[4]{0:T(128)} %bitcast.7, s32[4]{0:T(128)} %tile_block.1, bf16[4,256,256]{2,1,0:T(8,128)(2,1)} %flows.1, s32[4,128]{1,0:T(4,128)} %bitcast.6, s32[8,128]{1,0:T(8,128)} %bitcast.5), custom_call_target="tpu_custom_call" | custom-call | tf_op jit(solution)/shard_map/gravity/pallas_call | solution.py:495
  52.1 0.7 %publish.1 = (f32[4,128]{1,0:T(4,128)}, f32[8,128]{1,0:T(8,128)}, f32[128,128]{1,0:T(8,128)}) custom-call(f32[4,128]{1,0:T(4,128)S(1)} %get-tuple-element.9.a, f32[8,128]{1,0:T(8,128)S(1)} %get-tuple-element.10.b, f32[128,128]{1,0:T(8,128)S(1)} %get-tuple-element.11.g), custom_call_target="tpu_custom_call" | custom-call | tf_op jit(solution)/shard_map/publish/pallas_call | solution.py:542

commit v6 on v5

--- a/solution.py
+++ b/solution.py
@@ -40,14 +40,18 @@
 
 def kernel(
     dims,
-    routing,
-    tile_block,
+    routing_in,
+    tile_block_in,
     flows,
-    exp_ids,
-    imp_ids,
+    exp_ids_in,
+    imp_ids_in,
     a_out,
     b_out,
     g_out,
+    routing,
+    tile_block,
+    exp_ids,
+    imp_ids,
     fbuf,
     row_t,
     row_s,
@@ -130,13 +134,24 @@
     h_dev = [(after, lax.rem(m + k, Z)) for k in range(Z)], [(before, lax.rem(m + k, Z)) for k in range(Z)]
     xy = y * XN + x
 
+    operands = (
+        (tile_block_in, tile_block),
+        (routing_in, routing),
+        (exp_ids_in, exp_ids),
+        (imp_ids_in, imp_ids),
+        (flows, fbuf),
+    )
+    fetches = [pltpu.make_async_copy(src, dst, fsem.at[k]) for k, (src, dst) in enumerate(operands)]
+    for fetch in fetches:
+        fetch.start()
+
     barrier = pltpu.get_barrier_semaphore()
     greet = plane_dev + h_dev[0] + h_dev[1] + zc_dev
     for dev in greet:
         pl.semaphore_signal(barrier, inc=1, device_id=dev, device_id_type=MESH)
 
-    fcopy = pltpu.make_async_copy(flows, fbuf, fsem)
-    fcopy.start()
+    for fetch in fetches[:4]:
+        fetch.wait()
 
     def push(src, dst, sems, dev):
         pltpu.make_async_remote_copy(
@@ -363,7 +378,7 @@
                 mu[k] = keep(k, jnp.ones((SIDE, SIDE), F32))
                 return keep(k, fbuf[k].astype(F32) - 1.0)
 
-            fcopy.wait()
+            fetches[4].wait()
         else:
 
             def cells(k):
@@ -488,16 +503,19 @@
     chunk = NC // XY
     dma = pltpu.SemaphoreType.DMA
     vmem = functools.partial(pl.BlockSpec, memory_space=pltpu.VMEM)
-    smem = functools.partial(pl.BlockSpec, memory_space=pltpu.SMEM)
     cells = SLOTS * SIDE
     pair = (NC, NC)
     sems = [dma((4, 2))] * 4 + [dma((2,))] * 5
     a, b, g = pl.pallas_call(
         functools.partial(kernel, dims),
         out_shape=(pltpu.VMEM((4, NC), F32), pltpu.VMEM((8, NC), F32), pltpu.VMEM(pair, F32)),
-        in_specs=[smem(), smem(), pl.BlockSpec(memory_space=pl.ANY), vmem(), vmem()],
+        in_specs=[pl.BlockSpec(memory_space=pl.ANY)] * 5,
         out_specs=(vmem(), vmem(), vmem()),
         scratch_shapes=[
+            pltpu.SMEM((SLOTS,), jnp.int32),
+            pltpu.SMEM((routing.size,), jnp.int32),
+            pltpu.VMEM((4, NC), jnp.int32),
+            pltpu.VMEM((8, NC), jnp.int32),
             pltpu.VMEM((SLOTS, SIDE, SIDE), BF16),
             pltpu.VMEM((NC, cells), BF16),
             pltpu.VMEM((cells, NC), BF16),
@@ -527,7 +545,7 @@
             pltpu.VMEM((XY, 2, chunk, NC), F32),
             pltpu.VMEM((2 * Z, 2, chunk, NC), F32),
             pltpu.VMEM((XY, 2, chunk, NC), F32),
-            dma,
+            dma((5,)),
         ]
         + sems,
         compiler_params=pltpu.CompilerParams(collective_id=0, has_side_effects=True),

time: 52.9 us -> 52.1 us (0.985)
  Pallas kernels: 52.1 us -> 51.3 us
    pallas_call x1, Pallas kernels: 51.4 us -> 50.7 us  [per_device(): pl.pallas_call(functools.partial(kernel, dims), out_shape=(pltpu.VMEM((4,...]
where the time goes in v6:
time: 52.1 us; the launch traced here: 52 us
  Pallas kernels  51.3 us (98%)
  between operations  0.64 us (1%)
    pallas_call x1, Pallas kernels, per_device(): pl.pallas_call(functools.partial(kernel, dims), out_shape=(pltpu.VMEM((4,...  50.7 us

profile of v6, /device:TPU:1, one launch (start us, length us, event | category | flops | bytes accessed | tf_op | source)
XLA Modules:
  0.0 52.0 jit_solution(15939332385985476658)
XLA Ops:
  0.6 50.7 %gravity.1 = (f32[4,128]{1,0:T(4,128)S(1)}, f32[8,128]{1,0:T(8,128)S(1)}, f32[128,128]{1,0:T(8,128)S(1)}) custom-call(s32[4]{0:T(128)} %bitcast.7, s32[4]{0:T(128)} %tile_block_in.1, bf16[4,256,256]{2,1,0:T(8,128)(2,1)} %flows.1, s32[4,128]{1,0:T(4,128)} %bitcast.6, s32[8,128]{1,0:T(8,128)} %bitcast.5), custom_call_target="tpu_custom_call" | custom-call | tf_op jit(solution)/shard_map/gravity/pallas_call | solution.py:509
  51.3 0.7 %publish.1 = (f32[4,128]{1,0:T(4,128)}, f32[8,128]{1,0:T(8,128)}, f32[128,128]{1,0:T(8,128)}) custom-call(f32[4,128]{1,0:T(4,128)S(1)} %get-tuple-element.9.a, f32[8,128]{1,0:T(8,128)S(1)} %get-tuple-element.10.b, f32[128,128]{1,0:T(8,128)S(1)} %get-tuple-element.11.g), custom_call_target="tpu_custom_call" | custom-call | tf_op jit(solution)/shard_map/publish/pallas_call | solution.py:560

commit v7 on v6

--- a/solution.py
+++ b/solution.py
@@ -382,7 +382,7 @@
         else:
 
             def cells(k):
-                rate = keep(k, jnp.exp(c0 * x0[k] + c1 * (x0[k] - step * xq[k])))
+                rate = keep(k, jnp.exp(both * x0[k] - shrink * xq[k]))
                 mu[k] = rate
                 return keep(k, fbuf[k].astype(F32)) - rate
 
@@ -393,8 +393,8 @@
             table_store(r, table, arows)
             edge_store(r, table, arows)
             pl.semaphore_wait(barrier, len(greet))
+            rows_send(r)
             b_send(r)
-            rows_send(r)
             edge_send(r)
         else:
             b_send(r)
@@ -432,9 +432,12 @@
         scal_fan(r, far_dev)
         b_store(r + 1, bpart)
         b_send(r + 1)
+        table, arows = table_sums()
+        table_store(r + 1, table, arows)
+        rows_send(r + 1)
         scal_fan(r, mid_dev)
-        table, arows = table_sums()
-        table_send(r + 1, table, arows)
+        edge_store(r + 1, table, arows)
+        edge_send(r + 1)
         scal_fan(r, near_dev)
         if final:
             arrive(rsb.at[pl.ds(0, XY - 1)], rs_sem)
@@ -458,7 +461,7 @@
         quad = []
         for k in range(SLOTS):
             v = x0[k] - step * xq[k]
-            quad.append(fold(mu[k] * v * v))
+            quad.append(fold(mu[k] * (v * v)))
         qvec = (qa, qb, qg[...])
         res1 = (ra - step * qa, rb - step * qb, r0g[...] - step * qg[...])
         scal_store(r + 1, [inner(res1, res1), lanes(sum(quad)), inner(res1, qvec)])
@@ -473,6 +476,7 @@
         curve = curve + RIDGE * rr1 + 2.0 * beta * cross + beta * beta * rhr
         c1 = rr1 / curve
         c0 = step + c1 * beta
+        both, shrink = c0 + c1, c1 * step
         da = c0 * ra + c1 * (ra - step * qa)
         db = c0 * rb + c1 * (rb - step * qb)
         if not final:

time: 52.1 us -> 51.4 us (0.987)
  Pallas kernels: 51.3 us -> 50.7 us
    pallas_call x1, Pallas kernels: 50.7 us -> 50 us  [per_device(): pl.pallas_call(functools.partial(kernel, dims), out_shape=(pltpu.VMEM((4,...]
where the time goes in v7:
time: 51.4 us; the launch traced here: 51.3 us
  Pallas kernels  50.7 us (99%)
  between operations  0.64 us (1%)
    pallas_call x1, Pallas kernels, per_device(): pl.pallas_call(functools.partial(kernel, dims), out_shape=(pltpu.VMEM((4,...  50 us

profile of v7, /device:TPU:1, one launch (start us, length us, event | category | flops | bytes accessed | tf_op | source)
XLA Modules:
  0.0 51.3 jit_solution(17544427144819246007)
XLA Ops:
  0.6 50.0 %gravity.1 = (f32[4,128]{1,0:T(4,128)S(1)}, f32[8,128]{1,0:T(8,128)S(1)}, f32[128,128]{1,0:T(8,128)S(1)}) custom-call(s32[4]{0:T(128)} %bitcast.7, s32[4]{0:T(128)} %tile_block_in.1, bf16[4,256,256]{2,1,0:T(8,128)(2,1)} %flows.1, s32[4,128]{1,0:T(4,128)} %bitcast.6, s32[8,128]{1,0:T(8,128)} %bitcast.5), custom_call_target="tpu_custom_call" | custom-call | tf_op jit(solution)/shard_map/gravity/pallas_call | solution.py:513
  50.7 0.7 %publish.1 = (f32[4,128]{1,0:T(4,128)}, f32[8,128]{1,0:T(8,128)}, f32[128,128]{1,0:T(8,128)}) custom-call(f32[4,128]{1,0:T(4,128)S(1)} %get-tuple-element.9.a, f32[8,128]{1,0:T(8,128)S(1)} %get-tuple-element.10.b, f32[128,128]{1,0:T(8,128)S(1)} %get-tuple-element.11.g), custom_call_target="tpu_custom_call" | custom-call | tf_op jit(solution)/shard_map/publish/pallas_call | solution.py:564

commit v8 on v7

--- a/solution.py
+++ b/solution.py
@@ -355,9 +355,8 @@
         for (yy, xx), dev in zip(xy_at, xy_dev):
             push(tabs.at[:, pl.ds((yy * XN + xx) * chunk, chunk)], rsb.at[xy], rs_sem, dev)
 
-    def rows_out():
-        parts[pl.ds(me * own_rows, own_rows), :] = image[pl.ds(me * own_rows, own_rows), :]
-        for ee, mm in all_dev:
+    def rows_out(devs):
+        for ee, mm in devs:
             src = image.at[pl.ds((ee * Z + mm) * own_rows, own_rows)]
             push(src, parts.at[pl.ds(me * own_rows, own_rows)], part_sem, (ee, mm))
 
@@ -435,6 +434,9 @@
         table, arows = table_sums()
         table_store(r + 1, table, arows)
         rows_send(r + 1)
+        if final:
+            image[...] = table
+            rows_out(far_dev)
         scal_fan(r, mid_dev)
         edge_store(r + 1, table, arows)
         edge_send(r + 1)
@@ -443,8 +445,8 @@
             arrive(rsb.at[pl.ds(0, XY - 1)], rs_sem)
             rxb[zc] = sum(rsb[k] for k in range(XY))
             fan(rxb.at[zc], rx_sem, zc_dev)
-            image[...] = table
-            rows_out()
+            parts[pl.ds(me * own_rows, own_rows), :] = image[pl.ds(me * own_rows, own_rows), :]
+            rows_out(mid_dev + near_dev)
         qa = z_end(r + 1) + RIDGE * ra
         cols = columns(r + 1, qa)
         qgv = table_end(r + 1, table, cols) + RIDGE * r0g[...]

time: 51.4 us -> 51.4 us (level)
  no operation moved by 1% of the time
where the time goes in v8:
time: 51.4 us; the launch traced here: 51.3 us
  Pallas kernels  50.7 us (99%)
  between operations  0.64 us (1%)
    pallas_call x1, Pallas kernels, per_device(): pl.pallas_call(functools.partial(kernel, dims), out_shape=(pltpu.VMEM((4,...  50 us

profile of v8, /device:TPU:1, one launch (start us, length us, event | category | flops | bytes accessed | tf_op | source)
XLA Modules:
  0.0 51.3 jit_solution(4978378931746830707)
XLA Ops:
  0.6 50.0 %gravity.1 = (f32[4,128]{1,0:T(4,128)S(1)}, f32[8,128]{1,0:T(8,128)S(1)}, f32[128,128]{1,0:T(8,128)S(1)}) custom-call(s32[4]{0:T(128)} %bitcast.7, s32[4]{0:T(128)} %tile_block_in.1, bf16[4,256,256]{2,1,0:T(8,128)(2,1)} %flows.1, s32[4,128]{1,0:T(4,128)} %bitcast.6, s32[8,128]{1,0:T(8,128)} %bitcast.5), custom_call_target="tpu_custom_call" | custom-call | tf_op jit(solution)/shard_map/gravity/pallas_call | solution.py:515
  50.7 0.7 %publish.1 = (f32[4,128]{1,0:T(4,128)}, f32[8,128]{1,0:T(8,128)}, f32[128,128]{1,0:T(8,128)}) custom-call(f32[4,128]{1,0:T(4,128)S(1)} %get-tuple-element.9.a, f32[8,128]{1,0:T(8,128)S(1)} %get-tuple-element.10.b, f32[128,128]{1,0:T(8,128)S(1)} %get-tuple-element.11.g), custom_call_target="tpu_custom_call" | custom-call | tf_op jit(solution)/shard_map/publish/pallas_call | solution.py:566
